TPU v7x, 1024 devices: a whole 4x8x16 slice. The times are simulated.
1024 devices in a mesh: dp: 256 (over z, y, core), gz: 4 (over x).
Axes of the slice: x: 4, y: 8, z: 16, core: 2. Of those that a mesh axis runs over, the one named last changes fastest.
Arguments:
- features_in: bfloat16 [256, 32, 16, 512], P('dp', None, 'gz'), may hold values from -6 to 6
- kernel_taps: bfloat16 [27, 2048], replicated, may hold values from -0.21875 to 0.21875
- channel_bias: float32 [64], replicated, may hold values from -3 to 3
- upstream: bfloat16 [256, 64, 16, 512], P('dp', None, 'gz'), may hold values from -6 to 6
Outputs:
- output: bfloat16 [256, 64, 16, 512], P('dp', None, 'gz')
- grad_input: bfloat16 [256, 32, 16, 512], P('dp', None, 'gz')
- weight_grad: float32 [27, 2048], replicated
- bias_grad: float32 [64], replicated
All inputs are finite; a program needn't handle non-finite values.
Results may differ from a plain program's by a relative error of at most 0.0034.
Values may be sent and summed in bfloat16 or wider, within the bound.
No kernel may reach another device: no remote copies, remote signals or barrier semaphores. Data moves between devices by JAX's collectives and lax.ppermute only.
A program may use at most 32 MiB of HBM per device.

v0:
```python
import math

import jax
import jax.numpy as jnp
from jax import lax
from jax.sharding import Mesh
from jax.sharding import PartitionSpec as P

NX = 64
NY = 8
DP = ("dp_0", "dp_1", "dp_2")


def with_halo(cells, sides, width):
    for axis, dim in sides:
        count = lax.axis_size(axis)
        ends = count - 1
        head = lax.slice_in_dim(cells, 0, width, axis=dim)
        tail = lax.slice_in_dim(cells, cells.shape[dim] - width, cells.shape[dim], axis=dim)
        cells = jnp.concatenate(
            [
                lax.ppermute(tail, axis, [(i, (i + 1) % count) for i in range(ends)]),
                cells,
                lax.ppermute(head, axis, [((i + 1) % count, i) for i in range(ends)]),
            ],
            axis=dim,
        )
    return cells


def cut_along(shard, dim, length):
    before, after = (shard.shape[:dim], shard.shape[dim + 1 :])
    return jnp.moveaxis(shard.reshape(*before, length, -1, *after), dim, 0)


def sum_packed(arrays, axis, dims):
    length = lax.axis_size(axis)
    tiles = [cut_along(a, dim, length) for a, dim in zip(arrays, dims)]
    lines = jnp.concatenate([b.reshape(length, -1) for b in tiles], axis=1)
    width = max(16, -(-lines.shape[1] // 1024) * 8)
    lines = jnp.pad(lines, ((0, 0), (0, width * 128 - lines.shape[1]))).reshape(-1, 128)
    flat, at, outs = (lax.psum_scatter(lines, axis, tiled=True).reshape(-1), 0, [])
    for b in tiles:
        part = b[0]
        outs.append(flat[at : at + part.size].reshape(part.shape))
        at += part.size
    return tuple(outs)


def by_axis(shard, axes):
    for axis in axes:
        shard = lax.psum(shard, axis)
    return shard


def pad_sides(field):
    return jnp.pad(field, ((0, 0), (0, 0), (0, 0), (1, 1), (1, 1)))


def correlate(field, taps):
    return lax.conv_general_dilated(
        field,
        taps,
        (1, 1, 1),
        "VALID",
        dimension_numbers=("NCDHW", "DHWIO", "NCDHW"),
        preferred_element_type=jnp.float32,
    )


def on_device(features_in, kernel_taps, channel_bias, upstream):
    in_chan = features_in.shape[1]
    out_chan = upstream.shape[1]
    vol_count = features_in.shape[0]
    planes = features_in.shape[2]
    kernel = kernel_taps.reshape(3, 3, 3, in_chan, out_chan)
    flipped = jnp.transpose(kernel[::-1, ::-1, ::-1], (0, 1, 2, 4, 3))
    feats = features_in.reshape(vol_count, in_chan, planes, NY, NX)
    grads = upstream.reshape(vol_count, out_chan, planes, NY, NX)
    padded_in = pad_sides(with_halo(feats, (("gz", 2),), 1))
    padded_up = pad_sides(with_halo(grads, (("gz", 2),), 1))
    output = (correlate(padded_in, kernel) + channel_bias[None, :, None, None, None]).astype(
        jnp.bfloat16
    )
    grad_input = correlate(padded_up, flipped).astype(jnp.bfloat16)
    weight_term = lax.conv_general_dilated(
        padded_in,
        grads,
        (1, 1, 1),
        "VALID",
        dimension_numbers=("CNDHW", "IODHW", "DHWNC"),
        preferred_element_type=jnp.float32,
    )
    weight_term = weight_term.reshape(27, in_chan * out_chan)
    bias_term = jnp.sum(grads, axis=(0, 2, 3, 4), dtype=jnp.float32)
    cells_all = vol_count * lax.axis_size(DP) * planes * lax.axis_size("gz") * NY * NX
    factor = 1.0 / math.sqrt(cells_all)
    shares = sum_packed((weight_term, bias_term), "gz", (1, 0))
    summed = (by_axis(shares[0], DP), by_axis(shares[1], DP))
    weight_sum, bias_sum = (
        lax.all_gather(summed[0], "gz", axis=1, tiled=True),
        lax.all_gather(summed[1], "gz", axis=0, tiled=True),
    )
    output = output.reshape(vol_count, out_chan, planes, NY * NX)
    grad_input = grad_input.reshape(vol_count, in_chan, planes, NY * NX)
    return (output, grad_input, weight_sum * factor, bias_sum * factor)


def solution(mesh):
    split = Mesh(mesh.devices.reshape(16, 8, 2, mesh.shape["gz"]), ("dp_0", "dp_1", "dp_2", "gz"))
    placed = (P(DP, None, "gz", None), P(), P(), P(DP, None, "gz", None))
    return jax.shard_map(
        on_device,
        mesh=split,
        in_specs=placed,
        out_specs=(P(DP, None, "gz", None), P(DP, None, "gz", None), P(), P()),
        check_vma=False,
    )
```

profile of v0, /device:TPU:1, one launch (start us, length us, event | category | flops | bytes accessed | tf_op | source)
XLA Modules:
  0.0 211.4 jit_solution(8419715126115540510)
XLA Ops:
  7.2 1.1 reshape.83
  8.3 0.8 copy.62
  9.2 0.6 fusion.25
  9.7 3.9 %collective-permute-start = (bf16[1,32,1,8,64]{1,0,4,3,2:T(2,128)(2,1)S(1)}, bf16[1,32,1,8,64]{1,0,4,3,2:T(2,128)(2,1)S(1)}, u32[]{:S(2)}, u32[]{:S(2)}) collective-permute-start(bf16[1,32,1,8,64]{1,0,4,3,2:T(2,128)(2,1)S(1)} %get-tuple-element.22), channel_id=1, source_target_pairs={{0,1},{1,2},{2,3},{4,5},{5,6},{6,7},{8,9},{9,10},{10,11},{12,13},{... | collective-permute-start | bytes 98312 | tf_op jit(solution)/shard_map/ppermute | solution.py:22
  13.7 1.3 collective-permute-start.1
  15.1 0.3 reshape.49
  15.3 0.7 fusion.26
  16.1 4.6 %collective-permute-start.2 = (bf16[1,64,1,8,64]{4,3,1,2,0:T(8,128)(2,1)}, bf16[1,64,1,8,64]{4,3,1,2,0:T(8,128)(2,1)}, u32[]{:S(2)}, u32[]{:S(2)}) collective-permute-start(bf16[1,64,1,8,64]{4,3,1,2,0:T(8,128)(2,1)} %get-tuple-element.24), channel_id=1, source_target_pairs={{0,1},{1,2},{2,3},{4,5},{5,6},{6,7},{8,9},{9,10},{10,11},{12,13},{... | collective-permute-start | bytes 196616 | tf_op jit(solution)/shard_map/ppermute | solution.py:22
  20.7 1.3 collective-permute-start.3
  22.0 0.6 convert_reduce_fusion
  22.5 2.0 copy.77
  24.5 0.1 reshape.52
  24.6 0.9 reshape.47
  25.5 1.3 dynamic-slice
  27.5 7.0 %pad_maximum_fusion = bf16[1,32,6,8,64]{1,0,4,3,2:T(2,128)(2,1)S(1)} fusion(bf16[1,32,1,8,64]{1,0,4,3,2:T(2,128)(2,1)} %collective-permute-done.1, bf16[1,32,4,8,64]{1,0,4,3,2:T(2,128)(2,1)S(1)} %copy.62, bf16[1,32,1,8,64]{1,0,4,3,2:T(2,128)(2,1)S(1)} %collective-permute-done), kind=kLoop, calls=%fused_computation.4 | loop fusion | flops 196608 | bytes 393216 | tf_op jit(solution)/shard_map/concatenate | solution.py:20
  34.5 1.2 copy.65
  35.7 12.4 %fusion.27 = f32[3,3,3,32,64]{4,3,2,1,0:T(8,128)} fusion(bf16[1,32,6,8,64]{1,0,4,3,2:T(2,128)(2,1)S(1)} %pad_maximum_fusion, bf16[1,64,4,8,64]{1,0,4,3,2:T(2,128)(2,1)S(1)} %copy-done), kind=kOutput, calls=%fused_computation.38 | convolution fusion | flops 205455360 | bytes 679936 | tf_op jit(solution)/shard_map/conv_general_dilated | solution.py:86
  48.1 1.2 reshape_reshape.3
  49.3 0.8 reshape.53
  50.1 0.6 copy.86
  50.7 0.2 pad.9.clone
  51.0 0.1 copy.68
  51.1 0.1 slice.31
  51.1 0.7 copy-done.2
  51.9 2.6 %fusion.3 = bf16[4,8,8,9,64]{4,2,3,1,0:T(8,128)(2,1)S(1)} fusion(bf16[3,3,3,32,64]{4,3,2,1,0:T(8,128)(2,1)S(1)} %copy-done.2, bf16[32,6,8,1,7,2]{0,4,5,2,1,3:T(8,128)(2,1)S(1)} %slice.31, bf16[32,6,8,1,8,9]{0,4,5,2,1,3:T(8,128)(2,1)S(1)} %copy.68, f32[64]{0:T(128)S(1)} %copy-done.4, pred[8,9]{0,1:T(8,128)(4,1)S(1)} %copy-done.5), kind=kOutput, calls=%fused_computation.8 | convolution fusion | flops 234823680 | bytes 670024 | tf_op jit(solution)/shard_map/conv_general_dilated | solution.py:61
  54.5 0.1 copy.69
  54.6 1.0 copy.82
  55.6 1.0 reshape.84
  56.6 1.1 maximum_bitcast_fusion
  57.7 0.7 copy.87
  58.4 0.2 pad.11.clone
  58.6 0.1 copy.74
  58.7 0.1 slice.35
  58.8 4.3 %fusion.4 = bf16[4,8,8,9,32]{4,2,3,1,0:T(8,128)(2,1)S(1)} fusion(bf16[3,3,3,32,64]{4,3,2,1,0:T(8,128)(2,1)S(1)} %copy-done.2, bf16[64,6,8,1,7,2]{0,4,5,2,1,3:T(8,128)(2,1)S(1)} %slice.35, bf16[64,6,8,1,8,9]{0,4,5,2,1,3:T(8,128)(2,1)S(1)} %copy.74, pred[8,9]{0,1:T(8,128)(4,1)S(1)} %copy-done.5), kind=kOutput, calls=%fused_computation.9 | convolution fusion | flops 235339776 | bytes 786504 | tf_op jit(solution)/shard_map/conv_general_dilated | solution.py:61
  63.0 0.1 copy.75
  63.2 0.6 copy.83
  63.8 0.8 reshape.85
  64.6 25.4 %reduce-scatter.2.cloned.1.call-done = f32[112,128]{1,0:T(8,128)} async-done(((f32[448,128]{1,0:T(8,128)}), f32[112,128]{1,0:T(8,128)}) %reduce-scatter.2.cloned.1.call-update) | async-done | bytes 57360 | tf_op jit(solution)/shard_map/reduce_scatter | solution.py:42
  90.0 0.8 reshape.54
  90.9 0.7 slice.38
  91.5 44.9 %all-reduce.2 = (f32[27,512]{1,0:T(8,128)S(1)}, f32[16]{0:T(128)S(1)}) all-reduce(f32[27,512]{1,0:T(8,128)S(1)} %reshape.54, f32[16]{0:T(128)S(1)} %slice.38), channel_id=1, replica_groups=mesh['dp_0'=16,'dp_1'=8,'dp_2'=2,'gz'=4] {'dp_0'}, use_global_device_ids=true, to_apply=%region_2.3 | all-reduce | flops 13840 | bytes 110720 | tf_op jit(solution)/shard_map/psum | solution.py:52
  136.4 23.5 %all-reduce.3 = (f32[27,512]{1,0:T(8,128)S(1)}, f32[16]{0:T(128)S(1)}) all-reduce(f32[27,512]{1,0:T(8,128)S(1)} %get-tuple-element.16, f32[16]{0:T(128)S(1)} %get-tuple-element.17), channel_id=1, replica_groups=mesh['dp_0'=16,'dp_1'=8,'dp_2'=2,'gz'=4] {'dp_1'}, use_global_device_ids=true, to_apply=%region_3.4 | all-reduce | flops 13840 | bytes 110720 | tf_op jit(solution)/shard_map/psum | solution.py:52
  160.0 26.9 %all-reduce.4 = (f32[27,512]{1,0:T(8,128)S(1)}, f32[16]{0:T(128)S(1)}) all-reduce(f32[27,512]{1,0:T(8,128)S(1)} %get-tuple-element.18, f32[16]{0:T(128)S(1)} %get-tuple-element.19), channel_id=1, replica_groups=mesh['dp_0'=16,'dp_1'=8,'dp_2'=2,'gz'=4] {'dp_2'}, use_global_device_ids=true, to_apply=%region_4.5 | all-reduce | flops 13840 | bytes 110720 | tf_op jit(solution)/shard_map/psum | solution.py:52
  186.9 9.4 %all_gather.6 = f32[27,2048]{1,0:T(8,128)S(1)} all-gather(f32[27,512]{1,0:T(8,128)S(1)} %get-tuple-element.20), channel_id=1, replica_groups=mesh['dp_0'=16,'dp_1'=8,'dp_2'=2,'gz'=4] {'gz'}, dimensions={1}, use_global_device_ids=true | all-gather | bytes 276480 | tf_op jit(solution)/shard_map/all_gather | solution.py:101
  196.3 0.7 broadcast_multiply_fusion
  197.0 0.2 dynamic-update-slice
  197.2 6.9 %all-reduce.1 = f32[64]{0:T(128)S(1)} all-reduce(f32[64]{0:T(128)S(1)} %dynamic-update-slice), channel_id=1, replica_groups=mesh['dp_0'=16,'dp_1'=8,'dp_2'=2,'gz'=4] {'gz'}, use_global_device_ids=true, to_apply=%add.1 | all-reduce | flops 64 | bytes 512
  204.1 0.5 broadcast_multiply_fusion.1
  (22 shorter events, 0.3 us)
Async XLA Ops:
  7.2 82.9 %reduce-scatter.2.cloned.1.call-start = ((), (), s32[]{:S(2)}) async-start(), calls=%async_computation.1 | async-start | bytes 286720 | tf_op jit(solution)/shard_map/reduce_scatter | solution.py:42
  8.3 6.7 %copy-start.1 = (bf16[1,64,4,512]{3,2,1,0:T(4,128)(2,1)S(1)}, bf16[1,64,4,512]{3,2,1,0:T(4,128)(2,1)}, u32[]{:S(2)}) copy-start(bf16[1,64,4,512]{3,2,1,0:T(4,128)(2,1)} %param.7) | copy-start | bytes 786436
  9.7 17.7 %collective-permute-start = (bf16[1,32,1,8,64]{1,0,4,3,2:T(2,128)(2,1)S(1)}, bf16[1,32,1,8,64]{1,0,4,3,2:T(2,128)(2,1)S(1)}, u32[]{:S(2)}, u32[]{:S(2)}) collective-permute-start(bf16[1,32,1,8,64]{1,0,4,3,2:T(2,128)(2,1)S(1)} %get-tuple-element.22), channel_id=1, source_target_pairs={{0,1},{1,2},{2,3},{4,5},{5,6},{6,7},{8,9},{9,10},{10,11},{12,13},{... | collective-permute-start | bytes 98312 | tf_op jit(solution)/shard_map/ppermute | solution.py:22
  13.7 13.8 %collective-permute-start.1 = (bf16[1,32,1,8,64]{1,0,4,3,2:T(2,128)(2,1)S(1)}, bf16[1,32,1,8,64]{1,0,4,3,2:T(2,128)(2,1)}, u32[]{:S(2)}, u32[]{:S(2)}) collective-permute-start(bf16[1,32,1,8,64]{1,0,4,3,2:T(2,128)(2,1)S(1)} %get-tuple-element.23), channel_id=1, source_target_pairs={{1,0},{2,1},{3,2},{5,4},{6,5},{7,6},{9,8},{10,9},{11,10},{13,12},{... | collective-permute-start | bytes 98312 | tf_op jit(solution)/shard_map/ppermute | solution.py:24
  15.3 9.3 %copy-start.3 = (bf16[27,2048]{1,0:T(8,128)(2,1)S(1)}, bf16[27,2048]{1,0:T(8,128)(2,1)}, u32[]{:S(2)}) copy-start(bf16[27,2048]{1,0:T(8,128)(2,1)} %param.5) | copy-start | bytes 331780
  16.1 40.5 %collective-permute-start.2 = (bf16[1,64,1,8,64]{4,3,1,2,0:T(8,128)(2,1)}, bf16[1,64,1,8,64]{4,3,1,2,0:T(8,128)(2,1)}, u32[]{:S(2)}, u32[]{:S(2)}) collective-permute-start(bf16[1,64,1,8,64]{4,3,1,2,0:T(8,128)(2,1)} %get-tuple-element.24), channel_id=1, source_target_pairs={{0,1},{1,2},{2,3},{4,5},{5,6},{6,7},{8,9},{9,10},{10,11},{12,13},{... | collective-permute-start | bytes 196616 | tf_op jit(solution)/shard_map/ppermute | solution.py:22
  20.7 35.9 %collective-permute-start.3 = (bf16[1,64,1,8,64]{4,3,1,2,0:T(8,128)(2,1)}, bf16[1,64,1,8,64]{4,3,1,2,0:T(8,128)(2,1)}, u32[]{:S(2)}, u32[]{:S(2)}) collective-permute-start(bf16[1,64,1,8,64]{4,3,1,2,0:T(8,128)(2,1)} %get-tuple-element.25), channel_id=1, source_target_pairs={{1,0},{2,1},{3,2},{5,4},{6,5},{7,6},{9,8},{10,9},{11,10},{13,12},{... | collective-permute-start | bytes 196616 | tf_op jit(solution)/shard_map/ppermute | solution.py:24
  34.4 1.3 copy-start
  50.9 0.9 copy-start.2
  50.9 0.9 copy-start.4
  50.9 0.9 copy-start.5
Sparse Core Ops, SparseCore 0:
  50.3 39.7 reduce-scatter.1
where the time goes:
time: 215 us; the launch traced here: 211 us
  blocking collectives  112 us (52%)
  waiting for transfers between devices  25.4 us (12%)
  matrix products  19.2 us (9%)
  local copies, waits for them, and re-layouts  19 us (9%)
  between operations  15 us (7%)
  starting transfers between devices  11.2 us (5%)
  other arithmetic  9.97 us (5%)
    psum x3, blocking collectives, by_axis(): shard = lax.psum(shard, axis)  95.3 us
    reduce_scatter x1, waiting for transfers between devices, sum_packed(): lax.psum_scatter(lines, axis, tiled=True).reshape(-1)  25.4 us
    conv_general_dilated x1, matrix products, on_device(): lax.conv_general_dilated(padded_in, grads, (1, 1, 1), 'VALID', dimension_...  12.4 us
    all_gather x1, blocking collectives, on_device(): lax.all_gather(summed[0], 'gz', axis=1, tiled=True)  9.37 us
    ppermute x2, starting transfers between devices, with_halo(): lax.ppermute(tail, axis, [(i, (i + 1) % count) for i in range(ends)])  8.58 us
    concatenate x2, other arithmetic, with_halo(): jnp.concatenate([lax.ppermute(tail, axis, [(i, (i + 1) % count) for i in...  8.11 us
    unnamed x22, local copies, waits for them, and re-layouts  6.95 us
    unnamed x1, blocking collectives  6.9 us
  transfers between devices with their start and end apart: 5, of which 1 were waited for; matrix products, arithmetic and copies ran while one was open for 20% of the time, Pallas kernels for 0%

commit v1 on v0

--- a/solution.py
+++ b/solution.py
@@ -28,29 +28,19 @@
     return cells
 
 
-def cut_along(shard, dim, length):
-    before, after = (shard.shape[:dim], shard.shape[dim + 1 :])
-    return jnp.moveaxis(shard.reshape(*before, length, -1, *after), dim, 0)
+TILES = 64
+NEAR = ("dp_1", "dp_2", "gz")
 
 
-def sum_packed(arrays, axis, dims):
-    length = lax.axis_size(axis)
-    tiles = [cut_along(a, dim, length) for a, dim in zip(arrays, dims)]
-    lines = jnp.concatenate([b.reshape(length, -1) for b in tiles], axis=1)
-    width = max(16, -(-lines.shape[1] // 1024) * 8)
-    lines = jnp.pad(lines, ((0, 0), (0, width * 128 - lines.shape[1]))).reshape(-1, 128)
-    flat, at, outs = (lax.psum_scatter(lines, axis, tiled=True).reshape(-1), 0, [])
-    for b in tiles:
-        part = b[0]
-        outs.append(flat[at : at + part.size].reshape(part.shape))
-        at += part.size
-    return tuple(outs)
+def swap(blocks, axes):
+    return lax.all_to_all(blocks, axes, 0, 0, tiled=True)
 
 
-def by_axis(shard, axes):
-    for axis in axes:
-        shard = lax.psum(shard, axis)
-    return shard
+def sum_everywhere(tiles):
+    own = jnp.sum(swap(tiles, NEAR), axis=0)
+    far = lax.axis_size("dp_0")
+    own = jnp.sum(swap(jnp.broadcast_to(own, (far, *own.shape)), "dp_0"), axis=0)
+    return swap(jnp.broadcast_to(own, tiles.shape), NEAR)
 
 
 def pad_sides(field):
@@ -95,12 +85,11 @@
     bias_term = jnp.sum(grads, axis=(0, 2, 3, 4), dtype=jnp.float32)
     cells_all = vol_count * lax.axis_size(DP) * planes * lax.axis_size("gz") * NY * NX
     factor = 1.0 / math.sqrt(cells_all)
-    shares = sum_packed((weight_term, bias_term), "gz", (1, 0))
-    summed = (by_axis(shares[0], DP), by_axis(shares[1], DP))
-    weight_sum, bias_sum = (
-        lax.all_gather(summed[0], "gz", axis=1, tiled=True),
-        lax.all_gather(summed[1], "gz", axis=0, tiled=True),
-    )
+    rows = jnp.concatenate([weight_term, jnp.pad(bias_term[None], ((0, 4), (0, 2048 - out_chan)))])
+    tiles = rows.reshape(4, 8, 16, 128).transpose(0, 2, 1, 3).reshape(TILES, 8, 128)
+    total = sum_everywhere(tiles)
+    total = total.reshape(4, 16, 8, 128).transpose(0, 2, 1, 3).reshape(32, 2048)
+    weight_sum, bias_sum = (total[:27], total[27, :out_chan])
     output = output.reshape(vol_count, out_chan, planes, NY * NX)
     grad_input = grad_input.reshape(vol_count, in_chan, planes, NY * NX)
     return (output, grad_input, weight_sum * factor, bias_sum * factor)

time: 215 us -> 118 us (0.55); the launches traced: 211 us -> 117 us
  blocking collectives: 112 us -> 0 us
  starting transfers between devices: 11.2 us -> 54.9 us
  between operations: 15 us -> 0.93 us
  waiting for transfers between devices: 25.4 us -> 16.9 us
  local copies, waits for them, and re-layouts: 19 us -> 15.3 us
    psum x3 -> x0, blocking collectives: 95.3 us -> none  [by_axis(): shard = lax.psum(shard, axis)]
    all_to_all x0 -> x3, starting transfers between devices: none -> 44.3 us  [swap(): return lax.all_to_all(blocks, axes, 0, 0, tiled=True)]
    reduce_scatter x1 -> x0, waiting for transfers between devices: 25.4 us -> none  [sum_packed(): lax.psum_scatter(lines, axis, tiled=True).reshape(-1)]
    all_to_all x0 -> x3, waiting for transfers between devices: none -> 13.9 us  [swap(): return lax.all_to_all(blocks, axes, 0, 0, tiled=True)]
    all_gather x1 -> x0, blocking collectives: 9.37 us -> none  [on_device(): lax.all_gather(summed[0], 'gz', axis=1, tiled=True)]
    unnamed x1 -> x0, blocking collectives: 6.9 us -> none
    ppermute x2, waiting for transfers between devices: 0.01 us -> 3.02 us  [with_halo(): lax.ppermute(head, axis, [((i + 1) % count, i) for i in range(ends)])]
    unnamed x22 -> x19, local copies, waits for them, and re-layouts: 6.95 us -> 5.49 us
  transfers between devices with their start and end apart: 5 -> 7, of which waited for: 1 -> 4; matrix products, arithmetic and copies ran while one was open for 20% -> 17% of each run, Pallas kernels for 0% -> 0%
where the time goes in v1:
time: 118 us; the launch traced here: 117 us
  starting transfers between devices  54.9 us (47%)
  matrix products  18.5 us (16%)
  waiting for transfers between devices  16.9 us (14%)
  local copies, waits for them, and re-layouts  15.3 us (13%)
  other arithmetic  10.9 us (9%)
    all_to_all x3, starting transfers between devices, swap(): return lax.all_to_all(blocks, axes, 0, 0, tiled=True)  44.3 us
    all_to_all x3, waiting for transfers between devices, swap(): return lax.all_to_all(blocks, axes, 0, 0, tiled=True)  13.9 us
    conv_general_dilated x1, matrix products, on_device(): lax.conv_general_dilated(padded_in, grads, (1, 1, 1), 'VALID', dimension_...  11.8 us
    concatenate x2, other arithmetic, with_halo(): jnp.concatenate([lax.ppermute(tail, axis, [(i, (i + 1) % count) for i in...  8.28 us
    ppermute x2, starting transfers between devices, with_halo(): lax.ppermute(tail, axis, [(i, (i + 1) % count) for i in range(ends)])  7.85 us
    conv_general_dilated x2, matrix products, correlate(): lax.conv_general_dilated(field, taps, (1, 1, 1), 'VALID', dimension_numbe...  6.64 us
    unnamed x19, local copies, waits for them, and re-layouts  5.49 us
    ppermute x2, waiting for transfers between devices, with_halo(): lax.ppermute(head, axis, [((i + 1) % count, i) for i in range(ends)])  3.02 us
  transfers between devices with their start and end apart: 7, of which 4 were waited for; matrix products, arithmetic and copies ran while one was open for 17% of the time, Pallas kernels for 0%

profile of v1, /device:TPU:1, one launch (start us, length us, event | category | flops | bytes accessed | tf_op | source)
XLA Modules:
  0.0 117.5 jit_solution(6495117008321621068)
XLA Ops:
  0.6 1.1 reshape.78
  1.7 0.8 copy.62
  2.6 0.6 fusion.26
  3.2 3.9 %collective-permute-start = (bf16[1,32,1,8,64]{1,0,4,3,2:T(2,128)(2,1)S(1)}, bf16[1,32,1,8,64]{1,0,4,3,2:T(2,128)(2,1)S(1)}, u32[]{:S(2)}, u32[]{:S(2)}) collective-permute-start(bf16[1,32,1,8,64]{1,0,4,3,2:T(2,128)(2,1)S(1)} %get-tuple-element.16), channel_id=1, source_target_pairs={{0,1},{1,2},{2,3},{4,5},{5,6},{6,7},{8,9},{9,10},{10,11},{12,13},{... | collective-permute-start | bytes 98312 | tf_op jit(solution)/shard_map/ppermute | solution.py:22
  7.1 1.3 %collective-permute-start.1 = (bf16[1,32,1,8,64]{1,0,4,3,2:T(2,128)(2,1)S(1)}, bf16[1,32,1,8,64]{1,0,4,3,2:T(2,128)(2,1)}, u32[]{:S(2)}, u32[]{:S(2)}) collective-permute-start(bf16[1,32,1,8,64]{1,0,4,3,2:T(2,128)(2,1)S(1)} %get-tuple-element.17), channel_id=1, source_target_pairs={{1,0},{2,1},{3,2},{5,4},{6,5},{7,6},{9,8},{10,9},{11,10},{13,12},{... | collective-permute-start | bytes 98312 | tf_op jit(solution)/shard_map/ppermute | solution.py:24
  8.4 0.6 convert_reduce_fusion
  9.0 0.3 reshape.49
  9.3 2.0 %copy.77 = bf16[1,64,4,8,64]{1,0,4,3,2:T(2,128)(2,1)} copy(bf16[1,64,4,8,64]{4,3,1,2,0:T(8,128)(2,1)S(1)} %reshape.49) | data formatting | bytes 524288 | tf_op jit(solution)/shard_map/reshape | solution.py:69
  11.3 3.0 %collective-permute-done.1 = bf16[1,32,1,8,64]{1,0,4,3,2:T(2,128)(2,1)} collective-permute-done((bf16[1,32,1,8,64]{1,0,4,3,2:T(2,128)(2,1)S(1)}, bf16[1,32,1,8,64]{1,0,4,3,2:T(2,128)(2,1)}, u32[]{:S(2)}, u32[]{:S(2)}) %collective-permute-start.1) | collective-permute-done | bytes 32800 | tf_op jit(solution)/shard_map/ppermute | solution.py:24
  14.3 7.1 %pad_maximum_fusion = bf16[1,32,6,8,64]{1,0,4,3,2:T(2,128)(2,1)S(1)} fusion(bf16[1,32,1,8,64]{1,0,4,3,2:T(2,128)(2,1)} %collective-permute-done.1, bf16[1,32,4,8,64]{1,0,4,3,2:T(2,128)(2,1)S(1)} %copy.62, bf16[1,32,1,8,64]{1,0,4,3,2:T(2,128)(2,1)S(1)} %collective-permute-done), kind=kLoop, calls=%fused_computation.4 | loop fusion | flops 196608 | bytes 393216 | tf_op jit(solution)/shard_map/concatenate | solution.py:20
  21.5 11.8 %fusion.28 = f32[3,3,3,32,64]{4,3,2,1,0:T(8,128)S(1)} fusion(bf16[1,32,6,8,64]{1,0,4,3,2:T(2,128)(2,1)S(1)} %pad_maximum_fusion, bf16[1,64,4,8,64]{1,0,4,3,2:T(2,128)(2,1)S(1)} %copy-done), kind=kOutput, calls=%fused_computation.39 | convolution fusion | flops 205455360 | bytes 679936 | tf_op jit(solution)/shard_map/conv_general_dilated | solution.py:76
  33.3 0.1 reshape.51
  33.5 0.7 select_maximum_fusion
  34.2 16.7 %all-to-all-start = ((f32[64,8,128]{2,1,0:T(8,128)}), f32[64,8,128]{2,1,0:T(8,128)S(1)}, u32[]{:S(2)}, u32[]{:S(2)}) async-start(f32[64,8,128]{2,1,0:T(8,128)} %bitcast.13), calls=%async_computation | async-start | bytes 524288 | tf_op jit(solution)/shard_map/all_to_all | solution.py:36
  50.9 0.7 fusion.27
  51.6 3.9 %collective-permute-start.2 = (bf16[1,64,1,8,64]{4,3,1,2,0:T(8,128)(2,1)}, bf16[1,64,1,8,64]{4,3,1,2,0:T(8,128)(2,1)}, u32[]{:S(2)}, u32[]{:S(2)}) collective-permute-start(bf16[1,64,1,8,64]{4,3,1,2,0:T(8,128)(2,1)} %get-tuple-element.18), channel_id=1, source_target_pairs={{0,1},{1,2},{2,3},{4,5},{5,6},{6,7},{8,9},{9,10},{10,11},{12,13},{... | collective-permute-start | bytes 196616 | tf_op jit(solution)/shard_map/ppermute | solution.py:22
  55.5 1.5 %collective-permute-start.3 = (bf16[1,64,1,8,64]{4,3,1,2,0:T(8,128)(2,1)}, bf16[1,64,1,8,64]{4,3,1,2,0:T(8,128)(2,1)}, u32[]{:S(2)}, u32[]{:S(2)}) collective-permute-start(bf16[1,64,1,8,64]{4,3,1,2,0:T(8,128)(2,1)} %get-tuple-element.19), channel_id=1, source_target_pairs={{1,0},{2,1},{3,2},{5,4},{6,5},{7,6},{9,8},{10,9},{11,10},{13,12},{... | collective-permute-start | bytes 196616 | tf_op jit(solution)/shard_map/ppermute | solution.py:24
  57.0 0.9 reshape.47
  57.9 1.1 copy.65
  59.0 0.6 copy.86
  59.6 0.2 pad.9.clone
  59.8 0.0 copy-start.5
  59.8 0.1 copy.68
  59.9 0.1 slice.30
  60.0 0.7 copy-done.2
  60.7 2.4 %fusion.3 = bf16[4,8,8,9,64]{4,2,3,1,0:T(8,128)(2,1)S(1)} fusion(bf16[3,3,3,32,64]{4,3,2,1,0:T(8,128)(2,1)S(1)} %copy-done.2, bf16[32,6,8,1,7,2]{0,4,5,2,1,3:T(8,128)(2,1)S(1)} %slice.30, bf16[32,6,8,1,8,9]{0,4,5,2,1,3:T(8,128)(2,1)S(1)} %copy.68, f32[64]{0:T(128)S(1)} %copy-done.4, pred[8,9]{0,1:T(8,128)(4,1)S(1)} %copy-done.5), kind=kOutput, calls=%fused_computation.8 | convolution fusion | flops 234823680 | bytes 670024 | tf_op jit(solution)/shard_map/conv_general_dilated | solution.py:51
  63.1 0.1 copy.69
  63.2 0.1 all-to-all-done
  63.3 0.1 reduce_sum.28
  63.4 0.6 broadcast_in_dim.11
  64.0 15.1 %all-to-all-start.1 = ((f32[16,8,128]{2,1,0:T(8,128)}), f32[16,8,128]{2,1,0:T(8,128)S(1)}, u32[]{:S(2)}, u32[]{:S(2)}) async-start(f32[16,8,128]{2,1,0:T(8,128)} %broadcast_in_dim.11), calls=%async_computation.1 | async-start | bytes 131072 | tf_op jit(solution)/shard_map/all_to_all | solution.py:36
  79.2 1.0 copy.82
  80.1 1.0 reshape.79
  81.1 1.1 maximum_bitcast_fusion
  82.3 0.7 copy.87
  83.0 0.2 pad.11.clone
  83.2 0.1 copy.74
  83.3 0.1 slice.34
  83.3 7.4 %all-to-all-done.1 = f32[16,8,128]{2,1,0:T(8,128)S(1)} async-done(((f32[16,8,128]{2,1,0:T(8,128)}), f32[16,8,128]{2,1,0:T(8,128)S(1)}, u32[]{:S(2)}, u32[]{:S(2)}) %all-to-all-start.1) | async-done | bytes 65568 | tf_op jit(solution)/shard_map/all_to_all | solution.py:36
  90.7 0.7 broadcast_in_dim.12
  91.4 12.5 %all-to-all-start.2 = ((f32[64,8,128]{2,1,0:T(8,128)}), f32[64,8,128]{2,1,0:T(8,128)S(1)}, u32[]{:S(2)}, u32[]{:S(2)}) async-start(f32[64,8,128]{2,1,0:T(8,128)} %broadcast_in_dim.12), calls=%async_computation.2 | async-start | bytes 524288 | tf_op jit(solution)/shard_map/all_to_all | solution.py:36
  104.0 4.3 %fusion.4 = bf16[4,8,8,9,32]{4,2,3,1,0:T(8,128)(2,1)S(1)} fusion(bf16[3,3,3,32,64]{4,3,2,1,0:T(8,128)(2,1)S(1)} %copy-done.2, bf16[64,6,8,1,7,2]{0,4,5,2,1,3:T(8,128)(2,1)S(1)} %slice.34, bf16[64,6,8,1,8,9]{0,4,5,2,1,3:T(8,128)(2,1)S(1)} %copy.74, pred[8,9]{0,1:T(8,128)(4,1)S(1)} %copy-done.5), kind=kOutput, calls=%fused_computation.9 | convolution fusion | flops 235339776 | bytes 786504 | tf_op jit(solution)/shard_map/conv_general_dilated | solution.py:51
  108.2 0.1 copy.75
  108.4 0.6 copy.83
  109.0 0.8 reshape.80
  109.8 6.4 %all-to-all-done.2 = f32[64,8,128]{2,1,0:T(8,128)S(1)} async-done(((f32[64,8,128]{2,1,0:T(8,128)}), f32[64,8,128]{2,1,0:T(8,128)S(1)}, u32[]{:S(2)}, u32[]{:S(2)}) %all-to-all-start.2) | async-done | bytes 262176 | tf_op jit(solution)/shard_map/all_to_all | solution.py:36
  116.2 0.7 slice_multiply_fusion
  117.0 0.5 fusion.19
  (17 shorter events, 0.2 us)
Async XLA Ops:
  1.7 6.7 %copy-start.1 = (bf16[1,64,4,512]{3,2,1,0:T(4,128)(2,1)S(1)}, bf16[1,64,4,512]{3,2,1,0:T(4,128)(2,1)}, u32[]{:S(2)}) copy-start(bf16[1,64,4,512]{3,2,1,0:T(4,128)(2,1)} %param.7) | copy-start | bytes 786436
  3.2 8.2 %collective-permute-start = (bf16[1,32,1,8,64]{1,0,4,3,2:T(2,128)(2,1)S(1)}, bf16[1,32,1,8,64]{1,0,4,3,2:T(2,128)(2,1)S(1)}, u32[]{:S(2)}, u32[]{:S(2)}) collective-permute-start(bf16[1,32,1,8,64]{1,0,4,3,2:T(2,128)(2,1)S(1)} %get-tuple-element.16), channel_id=1, source_target_pairs={{0,1},{1,2},{2,3},{4,5},{5,6},{6,7},{8,9},{9,10},{10,11},{12,13},{... | collective-permute-start | bytes 98312 | tf_op jit(solution)/shard_map/ppermute | solution.py:22
  7.1 7.2 %collective-permute-start.1 = (bf16[1,32,1,8,64]{1,0,4,3,2:T(2,128)(2,1)S(1)}, bf16[1,32,1,8,64]{1,0,4,3,2:T(2,128)(2,1)}, u32[]{:S(2)}, u32[]{:S(2)}) collective-permute-start(bf16[1,32,1,8,64]{1,0,4,3,2:T(2,128)(2,1)S(1)} %get-tuple-element.17), channel_id=1, source_target_pairs={{1,0},{2,1},{3,2},{5,4},{6,5},{7,6},{9,8},{10,9},{11,10},{13,12},{... | collective-permute-start | bytes 98312 | tf_op jit(solution)/shard_map/ppermute | solution.py:24
  11.3 10.2 %copy-start = (bf16[1,64,4,8,64]{1,0,4,3,2:T(2,128)(2,1)S(1)}, bf16[1,64,4,8,64]{1,0,4,3,2:T(2,128)(2,1)}, u32[]{:S(2)}) copy-start(bf16[1,64,4,8,64]{1,0,4,3,2:T(2,128)(2,1)} %copy.77) | copy-start | bytes 786436
  33.3 23.7 %copy-start.3 = (bf16[27,2048]{1,0:T(8,128)(2,1)S(1)}, bf16[27,2048]{1,0:T(8,128)(2,1)}, u32[]{:S(2)}) copy-start(bf16[27,2048]{1,0:T(8,128)(2,1)} %param.5) | copy-start | bytes 331780
  34.2 29.1 %all-to-all-start = ((f32[64,8,128]{2,1,0:T(8,128)}), f32[64,8,128]{2,1,0:T(8,128)S(1)}, u32[]{:S(2)}, u32[]{:S(2)}) async-start(f32[64,8,128]{2,1,0:T(8,128)} %bitcast.13), calls=%async_computation | async-start | bytes 524288 | tf_op jit(solution)/shard_map/all_to_all | solution.py:36
  51.6 29.5 %collective-permute-start.2 = (bf16[1,64,1,8,64]{4,3,1,2,0:T(8,128)(2,1)}, bf16[1,64,1,8,64]{4,3,1,2,0:T(8,128)(2,1)}, u32[]{:S(2)}, u32[]{:S(2)}) collective-permute-start(bf16[1,64,1,8,64]{4,3,1,2,0:T(8,128)(2,1)} %get-tuple-element.18), channel_id=1, source_target_pairs={{0,1},{1,2},{2,3},{4,5},{5,6},{6,7},{8,9},{9,10},{10,11},{12,13},{... | collective-permute-start | bytes 196616 | tf_op jit(solution)/shard_map/ppermute | solution.py:22
  55.5 25.6 %collective-permute-start.3 = (bf16[1,64,1,8,64]{4,3,1,2,0:T(8,128)(2,1)}, bf16[1,64,1,8,64]{4,3,1,2,0:T(8,128)(2,1)}, u32[]{:S(2)}, u32[]{:S(2)}) collective-permute-start(bf16[1,64,1,8,64]{4,3,1,2,0:T(8,128)(2,1)} %get-tuple-element.19), channel_id=1, source_target_pairs={{1,0},{2,1},{3,2},{5,4},{6,5},{7,6},{9,8},{10,9},{11,10},{13,12},{... | collective-permute-start | bytes 196616 | tf_op jit(solution)/shard_map/ppermute | solution.py:24
  59.8 0.9 copy-start.2
  59.8 0.9 copy-start.4
  59.8 0.9 copy-start.5
  64.0 26.7 %all-to-all-start.1 = ((f32[16,8,128]{2,1,0:T(8,128)}), f32[16,8,128]{2,1,0:T(8,128)S(1)}, u32[]{:S(2)}, u32[]{:S(2)}) async-start(f32[16,8,128]{2,1,0:T(8,128)} %broadcast_in_dim.11), calls=%async_computation.1 | async-start | bytes 131072 | tf_op jit(solution)/shard_map/all_to_all | solution.py:36
  91.4 24.8 %all-to-all-start.2 = ((f32[64,8,128]{2,1,0:T(8,128)}), f32[64,8,128]{2,1,0:T(8,128)S(1)}, u32[]{:S(2)}, u32[]{:S(2)}) async-start(f32[64,8,128]{2,1,0:T(8,128)} %broadcast_in_dim.12), calls=%async_computation.2 | async-start | bytes 524288 | tf_op jit(solution)/shard_map/all_to_all | solution.py:36

commit v2 on v1

v2 whole, which is shorter than its diff:
```python
import functools
import math

import jax
import jax.numpy as jnp
from jax import lax
from jax.experimental import pallas as pl
from jax.experimental.pallas import tpu as pltpu
from jax.sharding import Mesh
from jax.sharding import PartitionSpec as P

NX = 64
NY = 8
DP = ("dp_0", "dp_1", "dp_2")
NEAR = ("dp_1", "dp_2", "gz")
TILES = 64
ROWS = 32
INTERPRET = False
VMEM = pl.BlockSpec(memory_space=pltpu.VMEM)


def on_core(body, out_shape, scratch=()):
    return pl.pallas_call(
        body,
        out_shape=out_shape,
        scratch_shapes=list(scratch),
        interpret=INTERPRET,
    )


def inside(width, db, dc):
    lane = lax.broadcasted_iota(jnp.int32, (1, width), 1)
    x = (lane & (NX - 1)) + dc
    y = lax.shift_right_logical(lane, NX.bit_length() - 1) + db
    return (x >= 0) & (x < NX) & (y >= 0) & (y < NY)


def moved(plane, b, c):
    width = plane.shape[-1]
    off = (b - 1) * NX + c - 1
    if off == 0:
        return plane
    return jnp.where(inside(width, b - 1, c - 1), pltpu.roll(plane, (-off) % width, 1), 0.0)


def store_moved(s_ref, at, plane):
    plane = plane.astype(jnp.float32)
    chans = plane.shape[0]
    for b in range(3):
        for c in range(3):
            row = at + (3 * b + c) * chans
            s_ref[row : row + chans, :] = moved(plane, b, c).astype(jnp.bfloat16)


def split_body(f_ref, u_ref, head_ref, mid_ref, tail_ref):
    cin, planes, _ = f_ref.shape
    for ref, at in ((f_ref, 0), (u_ref, cin)):
        rows = slice(at, at + ref.shape[0])
        own = jnp.swapaxes(ref[...].astype(jnp.float32), 0, 1).astype(jnp.bfloat16)
        head_ref[rows, :] = own[0]
        tail_ref[rows, :] = own[planes - 1]
        for z in range(1, planes - 1):
            mid_ref[z - 1, rows, :] = own[z]


def planes_of(head_ref, mid_ref, tail_ref, rows):
    mid = [mid_ref[z, rows, :] for z in range(mid_ref.shape[0])]
    return [head_ref[rows, :], *mid, tail_ref[rows, :]]


NT = (((1,), (1,)), ((), ()))


def dot(a, b, dims=(((1,), (0,)), ((), ()))):
    return lax.dot_general(a, b, dims, preferred_element_type=jnp.float32)


def own_body(cin, head_ref, mid_ref, tail_ref, w_ref, s_ref):
    width = head_ref.shape[1]
    cout = head_ref.shape[0] - cin
    taps = 9 * cin
    own = planes_of(head_ref, mid_ref, tail_ref, slice(0, cin))
    ups = planes_of(head_ref, mid_ref, tail_ref, slice(cin, cin + cout))
    planes = len(own)
    for z in range(planes):
        store_moved(s_ref, z * taps, own[z])
    twice = [jnp.concatenate([up, up], axis=0) for up in ups]
    for a in range(3):
        total = jnp.zeros((taps, 2 * cout), jnp.float32)
        for z in range(planes):
            src = z + a - 1
            if 0 <= src < planes:
                total += dot(s_ref[src * taps : (src + 1) * taps, :], twice[z], NT)
        w_ref[a * taps : (a + 1) * taps, :] = total
    ones = jnp.ones((16, width), jnp.bfloat16)
    bias = jnp.zeros((16, 2 * cout), jnp.float32)
    for z in range(planes):
        bias += dot(ones, twice[z], NT)
    w_ref[3 * taps :, :] = jnp.zeros((w_ref.shape[0] - 3 * taps, 2 * cout), jnp.float32)
    w_ref[3 * taps : 3 * taps + 8, :] = bias[:8]


def edge_body(cin, factor, lo_ref, head_ref, tail_ref, hi_ref, w_ref, tiles_ref, s_ref, v_ref):
    cout = lo_ref.shape[0] - cin
    taps = 9 * cin
    v_ref[...] = w_ref[...]
    for a, there_ref, here_ref in ((0, lo_ref, head_ref), (2, hi_ref, tail_ref)):
        at = a // 2 * taps
        store_moved(s_ref, at, there_ref[:cin, :])
        up = here_ref[cin:, :]
        twice = jnp.concatenate([up, up], axis=0)
        v_ref[a * taps : (a + 1) * taps, :] += dot(s_ref[at : at + taps, :], twice, NT)
    left = lax.broadcasted_iota(jnp.int32, (ROWS, 2 * cout), 1) < cout
    for at in range(cin // 2):
        even = v_ref[pl.ds(2 * at, ROWS, stride=cin), :]
        odd = v_ref[pl.ds(2 * at + 1, ROWS, stride=cin), :]
        tiles_ref[:, at] = (jnp.where(left, even, odd) * factor).reshape(ROWS // 8, 8, 2 * cout)


def forward_body(cin, lo_ref, head_ref, mid_ref, tail_ref, hi_ref, w_ref, bias_ref, out_ref, s_ref):
    taps = 9 * cin
    rows = slice(0, cin)
    slabs = [lo_ref[rows, :], *planes_of(head_ref, mid_ref, tail_ref, rows), hi_ref[rows, :]]
    for z, plane in enumerate(slabs):
        store_moved(s_ref, z * taps, plane)
    outs = [dot(w_ref[...], s_ref[z * taps : (z + 3) * taps, :]) + bias_ref[...] for z in range(len(slabs) - 2)]
    out_ref[...] = jnp.swapaxes(jnp.stack(outs), 0, 1).astype(jnp.bfloat16)


def backward_body(cin, lo_ref, head_ref, mid_ref, tail_ref, hi_ref, w_ref, _, out_ref, p_ref):
    width = lo_ref.shape[1]
    cout = lo_ref.shape[0] - cin
    rows = slice(cin, cin + cout)
    slabs = [lo_ref[rows, :], *planes_of(head_ref, mid_ref, tail_ref, rows), hi_ref[rows, :]]
    for z, plane in enumerate(slabs):
        p_ref[z * cout : (z + 1) * cout, :] = plane
    outs = []
    for z in range(len(slabs) - 2):
        parts = dot(w_ref[...], p_ref[z * cout : (z + 3) * cout, :])
        total = jnp.zeros((cin, width), jnp.float32)
        for b in range(3):
            for c in range(3):
                at = (3 * b + c) * cin
                total += moved(parts[at : at + cin], b, c)
        outs.append(total)
    out_ref[...] = jnp.swapaxes(jnp.stack(outs), 0, 1).astype(jnp.bfloat16)


def split_planes(feats, grads):
    planes, width = feats.shape[1:]
    rows = feats.shape[0] + grads.shape[0]
    one = jax.ShapeDtypeStruct((rows, width), feats.dtype)
    return on_core(split_body, (one, jax.ShapeDtypeStruct((planes - 2, rows, width), feats.dtype), one))(feats, grads)


def own_terms(cin, head, mid, tail):
    rows, width = head.shape
    planes = mid.shape[0] + 2
    return on_core(
        functools.partial(own_body, cin),
        jax.ShapeDtypeStruct((ROWS * cin, 2 * (rows - cin)), jnp.float32),
        [pltpu.VMEM((planes * 9 * cin, width), jnp.bfloat16)],
    )(head, mid, tail)


def weight_tiles(cin, lo, head, tail, hi, own, factor):
    rows, width = lo.shape
    return on_core(
        functools.partial(edge_body, cin, factor),
        jax.ShapeDtypeStruct((ROWS // 8, cin // 2, 8, 2 * (rows - cin)), jnp.float32),
        [pltpu.VMEM((18 * cin, width), jnp.bfloat16), pltpu.VMEM(own.shape, jnp.float32)],
    )(lo, head, tail, hi, own)


def forward(cin, slabs, taps, bias):
    rows, width = slabs[0].shape
    planes = slabs[2].shape[0] + 2
    return on_core(
        functools.partial(forward_body, cin),
        jax.ShapeDtypeStruct((rows - cin, planes, width), jnp.bfloat16),
        [pltpu.VMEM(((planes + 2) * 9 * cin, width), jnp.bfloat16)],
    )(*slabs, taps, bias)


def backward(cin, slabs, taps, after):
    rows, width = slabs[0].shape
    planes = slabs[2].shape[0] + 2
    return on_core(
        functools.partial(backward_body, cin),
        jax.ShapeDtypeStruct((cin, planes, width), jnp.bfloat16),
        [pltpu.VMEM(((planes + 2) * (rows - cin), width), jnp.bfloat16)],
    )(*slabs, taps, after)


def swap(blocks, axes):
    return lax.all_to_all(blocks, axes, 0, 0, tiled=True)


def on_device(features_in, kernel_taps, channel_bias, upstream):
    feats, grads = features_in[0], upstream[0]
    cin, depth, width = feats.shape
    cout = grads.shape[0]
    cells_all = lax.axis_size(DP) * depth * lax.axis_size("gz") * width
    factor = 1.0 / math.sqrt(cells_all)
    head, mid, tail = split_planes(feats, grads)
    slabs = lax.axis_size("gz")
    lo = lax.ppermute(tail, "gz", [(i, i + 1) for i in range(slabs - 1)])
    hi = lax.ppermute(head, "gz", [(i + 1, i) for i in range(slabs - 1)])
    planes = (lo, head, mid, tail, hi)
    kernel = kernel_taps.reshape(27, cin, cout)
    ahead = kernel.reshape(27 * cin, cout).T
    back = kernel[::-1].reshape(3, 9, cin, cout).transpose(1, 2, 0, 3).reshape(9 * cin, 3 * cout)
    own = own_terms(cin, head, mid, tail)
    tiles = weight_tiles(cin, lo, head, tail, hi, own, factor).reshape(TILES, 8, 128)
    part = jnp.sum(swap(tiles, NEAR), axis=0)
    output = forward(cin, planes, ahead, channel_bias[:, None])
    part, output = lax.optimization_barrier((part, output))
    grad_input = backward(cin, planes, back, part)
    far = lax.axis_size("dp_0")
    part = jnp.sum(swap(jnp.broadcast_to(part, (far, *part.shape)), "dp_0"), axis=0)
    part, grad_input = lax.optimization_barrier((part, grad_input))
    total = swap(jnp.broadcast_to(part, tiles.shape), NEAR)
    total = total.reshape(4, 16, 8, 128).transpose(0, 2, 1, 3).reshape(ROWS, 2048)
    return (output[None], grad_input[None], total[:27], total[27, :cout])


def solution(mesh):
    split = Mesh(mesh.devices.reshape(16, 8, 2, mesh.shape["gz"]), ("dp_0", "dp_1", "dp_2", "gz"))
    placed = (P(DP, None, "gz", None), P(), P(), P(DP, None, "gz", None))
    return jax.shard_map(
        on_device,
        mesh=split,
        in_specs=placed,
        out_specs=(P(DP, None, "gz", None), P(DP, None, "gz", None), P(), P()),
        check_vma=False,
    )
```

time: 118 us -> 91.5 us (0.78)
  blocking collectives: 0 us -> 19.3 us
  starting transfers between devices: 54.9 us -> 35.7 us
  matrix products: 18.5 us -> 0 us
  Pallas kernels: 0 us -> 13.1 us
  other arithmetic: 10.9 us -> 0.09 us
  local copies, waits for them, and re-layouts: 15.3 us -> 6.09 us
    all_to_all x0 -> x1, blocking collectives: none -> 19.3 us  [swap(): return lax.all_to_all(blocks, axes, 0, 0, tiled=True)]
    conv_general_dilated x3 -> x0, matrix products: 18.5 us -> none  [the longest x1 11.8 us: on_device(): lax.conv_general_dilated(padded_in, grads, (1, 1, 1), 'VALID', dimension_...]
    all_to_all x3 -> x2, starting transfers between devices: 44.3 us -> 30.5 us  [swap(): return lax.all_to_all(blocks, axes, 0, 0, tiled=True)]
    pallas_call x0 -> x5, Pallas kernels: none -> 13.1 us  [the longest x1 2.91 us: own_terms(): on_core(functools.partial(own_body, cin), jax.ShapeDtypeStruct((ROWS * ci...]
    concatenate x3 -> x0, other arithmetic: 9.01 us -> none  [the longest x2 8.28 us: with_halo(): jnp.concatenate([lax.ppermute(tail, axis, [(i, (i + 1) % count) for i in...]
    ppermute x4 -> x2, starting transfers between devices: 10.6 us -> 5.22 us  [the longest x1 3.93 us: on_device(): lo = lax.ppermute(tail, 'gz', [(i, i + 1) for i in range(slabs - 1)])]
    reshape x6 -> x2, local copies, waits for them, and re-layouts: 5.23 us -> 1.07 us  [the longest x1 0.87 us: on_device(): kernel[::-1].reshape(3, 9, cin, cout).transpose(1, 2, 0, 3)]
    unnamed x19 -> x11, local copies, waits for them, and re-layouts: 5.49 us -> 2 us
  transfers between devices with their start and end apart: 7 -> 4, of which waited for: 4 -> 3; matrix products, arithmetic and copies ran while one was open for 17% -> 3% of each run, Pallas kernels for 0% -> 9%
where the time goes in v2:
time: 91.5 us; the launch traced here: 91 us
  starting transfers between devices  35.7 us (39%)
  blocking collectives  19.3 us (21%)
  waiting for transfers between devices  16 us (17%)
  Pallas kernels  13.1 us (14%)
  local copies, waits for them, and re-layouts  6.09 us (7%)
    all_to_all x2, starting transfers between devices, swap(): return lax.all_to_all(blocks, axes, 0, 0, tiled=True)  30.5 us
    all_to_all x1, blocking collectives, swap(): return lax.all_to_all(blocks, axes, 0, 0, tiled=True)  19.3 us
    all_to_all x2, waiting for transfers between devices, swap(): return lax.all_to_all(blocks, axes, 0, 0, tiled=True)  14.7 us
    ppermute x1, starting transfers between devices, on_device(): lo = lax.ppermute(tail, 'gz', [(i, i + 1) for i in range(slabs - 1)])  3.93 us
    pallas_call x1, Pallas kernels, own_terms(): on_core(functools.partial(own_body, cin), jax.ShapeDtypeStruct((ROWS * ci...  2.91 us
    pallas_call x1, Pallas kernels, forward(): on_core(functools.partial(forward_body, cin), jax.ShapeDtypeStruct((rows...  2.89 us
    pallas_call x1, Pallas kernels, backward(): on_core(functools.partial(backward_body, cin), jax.ShapeDtypeStruct((cin,...  2.77 us
    pallas_call x1, Pallas kernels, weight_tiles(): on_core(functools.partial(edge_body, cin, factor), jax.ShapeDtypeStruct((...  2.55 us
  transfers between devices with their start and end apart: 4, of which 3 were waited for; matrix products, arithmetic and copies ran while one was open for 3% of the time, Pallas kernels for 9%

profile of v2, /device:TPU:1, one launch (start us, length us, event | category | flops | bytes accessed | tf_op | source)
XLA Modules:
  0.0 91.0 jit_solution(4724397753426861307)
XLA Ops:
  0.6 1.9 %shard_map.75 = (bf16[96,512]{1,0:T(8,128)(2,1)}, bf16[2,96,512]{2,1,0:T(8,128)(2,1)}, bf16[96,512]{1,0:T(8,128)(2,1)}) custom-call(bf16[32,4,512]{2,1,0:T(4,128)(2,1)} %bitcast.25, bf16[64,4,512]{2,1,0:T(4,128)(2,1)} %bitcast.23), custom_call_target="tpu_custom_call" | custom-call | tf_op jit(solution)/shard_map/pallas_call | solution.py:153
  2.6 3.9 %collective-permute-start = (bf16[96,512]{1,0:T(8,128)(2,1)}, bf16[96,512]{1,0:T(8,128)(2,1)S(1)}, u32[]{:S(2)}, u32[]{:S(2)}) collective-permute-start(bf16[96,512]{1,0:T(8,128)(2,1)} %get-tuple-element.11.tail_ref), channel_id=1, source_target_pairs={{0,1},{1,2},{2,3},{4,5},{5,6},{6,7},{8,9},{9,10},{10,11},{12,13},{... | collective-permute-start | bytes 294920 | tf_op jit(solution)/shard_map/ppermute | solution.py:207
  6.5 1.3 %collective-permute-start.1 = (bf16[96,512]{1,0:T(8,128)(2,1)}, bf16[96,512]{1,0:T(8,128)(2,1)S(1)}, u32[]{:S(2)}, u32[]{:S(2)}) collective-permute-start(bf16[96,512]{1,0:T(8,128)(2,1)} %get-tuple-element.12.head_ref), channel_id=1, source_target_pairs={{1,0},{2,1},{3,2},{5,4},{6,5},{7,6},{9,8},{10,9},{11,10},{13,12},{... | collective-permute-start | bytes 294920 | tf_op jit(solution)/shard_map/ppermute | solution.py:208
  7.8 2.9 %shard_map.76.w_ref = f32[1024,128]{1,0:T(8,128)} custom-call(bf16[96,512]{1,0:T(8,128)(2,1)} %get-tuple-element.12.head_ref, bf16[2,96,512]{2,1,0:T(8,128)(2,1)} %get-tuple-element.13.mid_ref, bf16[96,512]{1,0:T(8,128)(2,1)} %get-tuple-element.11.tail_ref), custom_call_target="tpu_custom_call" | custom-call | tf_op jit(solution)/shard_map/pallas_call | solution.py:159
  10.7 0.0 collective-permute-done.lo_ref
  10.7 0.0 copy-start
  10.7 1.4 %collective-permute-done.1.hi_ref = bf16[96,512]{1,0:T(8,128)(2,1)S(1)} collective-permute-done((bf16[96,512]{1,0:T(8,128)(2,1)}, bf16[96,512]{1,0:T(8,128)(2,1)S(1)}, u32[]{:S(2)}, u32[]{:S(2)}) %collective-permute-start.1) | collective-permute-done | bytes 98336 | tf_op jit(solution)/shard_map/ppermute | solution.py:208
  12.1 0.0 copy-done
  12.1 0.0 copy-start.1
  12.1 0.6 copy-done.1
  12.7 2.6 %shard_map.77 = f32[4,16,8,128]{3,2,1,0:T(8,128)} custom-call(bf16[96,512]{1,0:T(8,128)(2,1)} %copy-done, bf16[96,512]{1,0:T(8,128)(2,1)} %get-tuple-element.12.head_ref, bf16[96,512]{1,0:T(8,128)(2,1)} %get-tuple-element.11.tail_ref, bf16[96,512]{1,0:T(8,128)(2,1)} %copy-done.1, f32[1024,128]{1,0:T(8,128)} %shard_map.76.w_ref), custom_call_target="tpu_custom_call" | custom-call | tf_op jit(solution)/shard_map/pallas_call | solution.py:168
  15.3 0.0 copy-start.2
  15.3 16.8 %all-to-all-start = ((f32[64,8,128]{2,1,0:T(8,128)}), f32[64,8,128]{2,1,0:T(8,128)S(1)}, u32[]{:S(2)}, u32[]{:S(2)}) async-start(f32[64,8,128]{2,1,0:T(8,128)} %bitcast.20), calls=%async_computation | async-start | bytes 524288 | tf_op jit(solution)/shard_map/all_to_all | solution.py:196
  32.1 0.0 copy-done.2
  32.1 0.2 reshape_reshape.3
  32.3 0.8 copy.12
  33.1 0.0 copy-start.4
  33.1 0.7 copy-done.4
  33.8 0.7 copy.13.bias_ref
  34.5 2.9 %shard_map.78 = bf16[64,4,512]{2,1,0:T(4,128)(2,1)} custom-call(bf16[96,512]{1,0:T(8,128)(2,1)} %copy-done, bf16[96,512]{1,0:T(8,128)(2,1)} %get-tuple-element.12.head_ref, bf16[2,96,512]{2,1,0:T(8,128)(2,1)} %get-tuple-element.13.mid_ref, bf16[96,512]{1,0:T(8,128)(2,1)} %get-tuple-element.11.tail_ref, bf16[96,512]{1,0:T(8,128)(2,1)} %copy-done.1, ...), custom_call_target="tpu_custom_call" | custom-call | tf_op jit(solution)/shard_map/pallas_call | solution.py:178
  37.4 7.2 %all-to-all-done = f32[64,8,128]{2,1,0:T(8,128)S(1)} async-done(((f32[64,8,128]{2,1,0:T(8,128)}), f32[64,8,128]{2,1,0:T(8,128)S(1)}, u32[]{:S(2)}, u32[]{:S(2)}) %all-to-all-start) | async-done | bytes 262176 | tf_op jit(solution)/shard_map/all_to_all | solution.py:196
  44.5 0.1 reduce_sum.18._
  44.6 0.0 copy-start.3
  44.6 0.6 broadcast_in_dim.17
  45.2 0.0 copy-done.3
  45.2 13.7 %all-to-all-start.1 = ((f32[16,8,128]{2,1,0:T(8,128)}), f32[16,8,128]{2,1,0:T(8,128)S(1)}, u32[]{:S(2)}, u32[]{:S(2)}) async-start(f32[16,8,128]{2,1,0:T(8,128)} %broadcast_in_dim.17), calls=%async_computation.1 | async-start | bytes 131072 | tf_op jit(solution)/shard_map/all_to_all | solution.py:196
  58.9 0.2 reshape.27
  59.1 0.2 copy.14
  59.3 0.9 reshape.29.w_ref
  60.2 2.8 %shard_map.79 = bf16[32,4,512]{2,1,0:T(4,128)(2,1)} custom-call(bf16[96,512]{1,0:T(8,128)(2,1)} %copy-done, bf16[96,512]{1,0:T(8,128)(2,1)} %get-tuple-element.12.head_ref, bf16[2,96,512]{2,1,0:T(8,128)(2,1)} %get-tuple-element.13.mid_ref, bf16[96,512]{1,0:T(8,128)(2,1)} %get-tuple-element.11.tail_ref, bf16[96,512]{1,0:T(8,128)(2,1)} %copy-done.1, ...), custom_call_target="tpu_custom_call" | custom-call | tf_op jit(solution)/shard_map/pallas_call | solution.py:188
  63.0 7.5 %all-to-all-done.1 = f32[16,8,128]{2,1,0:T(8,128)S(1)} async-done(((f32[16,8,128]{2,1,0:T(8,128)}), f32[16,8,128]{2,1,0:T(8,128)S(1)}, u32[]{:S(2)}, u32[]{:S(2)}) %all-to-all-start.1) | async-done | bytes 65568 | tf_op jit(solution)/shard_map/all_to_all | solution.py:196
  70.5 19.3 %all_to_all.15 = f32[64,8,128]{2,1,0:T(8,128)S(1)} all-to-all(f32[64,8,128]{2,1,0:T(8,128)S(1)} %broadcast_in_dim.19), channel_id=1, replica_groups=mesh['dp_0'=16,'dp_1'=8,'dp_2'=2,'gz'=4] {'dp_1','dp_2','gz'}, dimensions={0} | all-to-all | bytes 524288 | tf_op jit(solution)/shard_map/all_to_all | solution.py:196
  89.8 0.5 slice_bitcast_fusion
  90.3 0.7 copy.16
  (3 shorter events, 0.1 us)
Async XLA Ops:
  2.6 8.1 %collective-permute-start = (bf16[96,512]{1,0:T(8,128)(2,1)}, bf16[96,512]{1,0:T(8,128)(2,1)S(1)}, u32[]{:S(2)}, u32[]{:S(2)}) collective-permute-start(bf16[96,512]{1,0:T(8,128)(2,1)} %get-tuple-element.11.tail_ref), channel_id=1, source_target_pairs={{0,1},{1,2},{2,3},{4,5},{5,6},{6,7},{8,9},{9,10},{10,11},{12,13},{... | collective-permute-start | bytes 294920 | tf_op jit(solution)/shard_map/ppermute | solution.py:207
  6.5 5.6 %collective-permute-start.1 = (bf16[96,512]{1,0:T(8,128)(2,1)}, bf16[96,512]{1,0:T(8,128)(2,1)S(1)}, u32[]{:S(2)}, u32[]{:S(2)}) collective-permute-start(bf16[96,512]{1,0:T(8,128)(2,1)} %get-tuple-element.12.head_ref), channel_id=1, source_target_pairs={{1,0},{2,1},{3,2},{5,4},{6,5},{7,6},{9,8},{10,9},{11,10},{13,12},{... | collective-permute-start | bytes 294920 | tf_op jit(solution)/shard_map/ppermute | solution.py:208
  10.7 1.4 %copy-start = (bf16[96,512]{1,0:T(8,128)(2,1)}, bf16[96,512]{1,0:T(8,128)(2,1)S(1)}, u32[]{:S(2)}) copy-start(bf16[96,512]{1,0:T(8,128)(2,1)S(1)} %collective-permute-done.lo_ref) | copy-start | bytes 294916
  12.1 0.6 copy-start.1
  15.3 16.8 %copy-start.2 = (bf16[27,2048]{1,0:T(8,128)(2,1)S(1)}, bf16[27,2048]{1,0:T(8,128)(2,1)}, u32[]{:S(2)}) copy-start(bf16[27,2048]{1,0:T(8,128)(2,1)} %param.5) | copy-start | bytes 331780
  15.3 29.2 %all-to-all-start = ((f32[64,8,128]{2,1,0:T(8,128)}), f32[64,8,128]{2,1,0:T(8,128)S(1)}, u32[]{:S(2)}, u32[]{:S(2)}) async-start(f32[64,8,128]{2,1,0:T(8,128)} %bitcast.20), calls=%async_computation | async-start | bytes 524288 | tf_op jit(solution)/shard_map/all_to_all | solution.py:196
  33.1 0.7 copy-start.4
  44.6 0.6 copy-start.3
  45.2 25.3 %all-to-all-start.1 = ((f32[16,8,128]{2,1,0:T(8,128)}), f32[16,8,128]{2,1,0:T(8,128)S(1)}, u32[]{:S(2)}, u32[]{:S(2)}) async-start(f32[16,8,128]{2,1,0:T(8,128)} %broadcast_in_dim.17), calls=%async_computation.1 | async-start | bytes 131072 | tf_op jit(solution)/shard_map/all_to_all | solution.py:196

commit v3 on v2

--- a/solution.py
+++ b/solution.py
@@ -19,13 +19,20 @@
 VMEM = pl.BlockSpec(memory_space=pltpu.VMEM)
 
 
-def on_core(body, out_shape, scratch=()):
-    return pl.pallas_call(
-        body,
-        out_shape=out_shape,
-        scratch_shapes=list(scratch),
-        interpret=INTERPRET,
-    )
+def on_core(body, out_shape, scratch=(), held=True, near=True):
+    def call(*operands):
+        if held:
+            operands = [pltpu.with_memory_space_constraint(x, pltpu.VMEM) for x in operands]
+        return pl.pallas_call(
+            body,
+            out_shape=jax.tree.map(lambda s: pltpu.VMEM(s.shape, s.dtype), out_shape) if near else out_shape,
+            in_specs=[VMEM] * len(operands),
+            out_specs=jax.tree.map(lambda _: VMEM, out_shape),
+            scratch_shapes=list(scratch),
+            interpret=INTERPRET,
+        )(*operands)
+
+    return call
 
 
 def inside(width, db, dc):
@@ -150,7 +157,8 @@
     planes, width = feats.shape[1:]
     rows = feats.shape[0] + grads.shape[0]
     one = jax.ShapeDtypeStruct((rows, width), feats.dtype)
-    return on_core(split_body, (one, jax.ShapeDtypeStruct((planes - 2, rows, width), feats.dtype), one))(feats, grads)
+    mid = jax.ShapeDtypeStruct((planes - 2, rows, width), feats.dtype)
+    return on_core(split_body, (one, mid, one), held=False)(feats, grads)
 
 
 def own_terms(cin, head, mid, tail):
@@ -179,6 +187,7 @@
         functools.partial(forward_body, cin),
         jax.ShapeDtypeStruct((rows - cin, planes, width), jnp.bfloat16),
         [pltpu.VMEM(((planes + 2) * 9 * cin, width), jnp.bfloat16)],
+        near=False,
     )(*slabs, taps, bias)
 
 
@@ -189,6 +198,7 @@
         functools.partial(backward_body, cin),
         jax.ShapeDtypeStruct((cin, planes, width), jnp.bfloat16),
         [pltpu.VMEM(((planes + 2) * (rows - cin), width), jnp.bfloat16)],
+        near=False,
     )(*slabs, taps, after)
 
 
@@ -219,7 +229,7 @@
     far = lax.axis_size("dp_0")
     part = jnp.sum(swap(jnp.broadcast_to(part, (far, *part.shape)), "dp_0"), axis=0)
     part, grad_input = lax.optimization_barrier((part, grad_input))
-    total = swap(jnp.broadcast_to(part, tiles.shape), NEAR)
+    total = swap(jnp.broadcast_to(part.astype(jnp.bfloat16), tiles.shape), NEAR).astype(jnp.float32)
     total = total.reshape(4, 16, 8, 128).transpose(0, 2, 1, 3).reshape(ROWS, 2048)
     return (output[None], grad_input[None], total[:27], total[27, :cout])
 

time: 91.5 us -> 85.9 us (0.939)
  Pallas kernels: 13.1 us -> 6.84 us
  waiting for transfers between devices: 16 us -> 22 us
  local copies, waits for them, and re-layouts: 6.09 us -> 3.03 us
  blocking collectives: 19.3 us -> 17.1 us
    pallas_call x5, Pallas kernels: 13.1 us -> 6.84 us  [call(): pl.pallas_call(body, out_shape=jax.tree.map(lambda s: pltpu.VMEM(s.shape,...]
    all_to_all x2, waiting for transfers between devices: 14.7 us -> 19 us  [swap(): return lax.all_to_all(blocks, axes, 0, 0, tiled=True)]
    all_to_all x1, blocking collectives: 19.3 us -> 17.1 us  [swap(): return lax.all_to_all(blocks, axes, 0, 0, tiled=True)]
    ppermute x1, waiting for transfers between devices: 1.36 us -> 2.98 us  [on_device(): hi = lax.ppermute(head, 'gz', [(i + 1, i) for i in range(slabs - 1)])]
    unnamed x11 -> x6, local copies, waits for them, and re-layouts: 2 us -> 0.8 us
  transfers between devices with their start and end apart: 4 -> 4, of which waited for: 3 -> 3; matrix products, arithmetic and copies ran while one was open for 3% -> 1% of each run, Pallas kernels for 9% -> 5%
where the time goes in v3:
time: 85.9 us; the launch traced here: 85.5 us
  starting transfers between devices  35.8 us (42%)
  waiting for transfers between devices  22 us (26%)
  blocking collectives  17.1 us (20%)
  Pallas kernels  6.84 us (8%)
  local copies, waits for them, and re-layouts  3.03 us (4%)
    all_to_all x2, starting transfers between devices, swap(): return lax.all_to_all(blocks, axes, 0, 0, tiled=True)  30.5 us
    all_to_all x2, waiting for transfers between devices, swap(): return lax.all_to_all(blocks, axes, 0, 0, tiled=True)  19 us
    all_to_all x1, blocking collectives, swap(): return lax.all_to_all(blocks, axes, 0, 0, tiled=True)  17.1 us
    pallas_call x5, Pallas kernels, call(): pl.pallas_call(body, out_shape=jax.tree.map(lambda s: pltpu.VMEM(s.shape,...  6.84 us
    ppermute x1, starting transfers between devices, on_device(): lo = lax.ppermute(tail, 'gz', [(i, i + 1) for i in range(slabs - 1)])  3.94 us
    ppermute x1, waiting for transfers between devices, on_device(): hi = lax.ppermute(head, 'gz', [(i + 1, i) for i in range(slabs - 1)])  2.98 us
  transfers between devices with their start and end apart: 4, of which 3 were waited for; matrix products, arithmetic and copies ran while one was open for 1% of the time, Pallas kernels for 5%

profile of v3, /device:TPU:1, one launch (start us, length us, event | category | flops | bytes accessed | tf_op | source)
XLA Modules:
  0.0 85.5 jit_solution(12435300998443780762)
XLA Ops:
  0.6 1.2 %shard_map.75 = (bf16[96,512]{1,0:T(8,128)(2,1)S(1)}, bf16[2,96,512]{2,1,0:T(8,128)(2,1)S(1)}, bf16[96,512]{1,0:T(8,128)(2,1)S(1)}) custom-call(bf16[32,4,512]{2,1,0:T(4,128)(2,1)} %bitcast.25, bf16[64,4,512]{2,1,0:T(4,128)(2,1)} %bitcast.22), custom_call_target="tpu_custom_call" | custom-call | tf_op jit(solution)/shard_map/pallas_call | solution.py:26
  1.8 3.9 %collective-permute-start = (bf16[96,512]{1,0:T(8,128)(2,1)S(1)}, bf16[96,512]{1,0:T(8,128)(2,1)S(1)}, u32[]{:S(2)}, u32[]{:S(2)}) collective-permute-start(bf16[96,512]{1,0:T(8,128)(2,1)S(1)} %get-tuple-element.11.tail_ref), channel_id=1, source_target_pairs={{0,1},{1,2},{2,3},{4,5},{5,6},{6,7},{8,9},{9,10},{10,11},{12,13},{... | collective-permute-start | bytes 294920 | tf_op jit(solution)/shard_map/ppermute | solution.py:217
  5.8 1.3 %collective-permute-start.1 = (bf16[96,512]{1,0:T(8,128)(2,1)S(1)}, bf16[96,512]{1,0:T(8,128)(2,1)S(1)}, u32[]{:S(2)}, u32[]{:S(2)}) collective-permute-start(bf16[96,512]{1,0:T(8,128)(2,1)S(1)} %get-tuple-element.12.head_ref), channel_id=1, source_target_pairs={{1,0},{2,1},{3,2},{5,4},{6,5},{7,6},{9,8},{10,9},{11,10},{13,12},{... | collective-permute-start | bytes 294920 | tf_op jit(solution)/shard_map/ppermute | solution.py:218
  7.1 1.1 %shard_map.76.w_ref = f32[1024,128]{1,0:T(8,128)S(1)} custom-call(bf16[96,512]{1,0:T(8,128)(2,1)S(1)} %get-tuple-element.12.head_ref, bf16[2,96,512]{2,1,0:T(8,128)(2,1)S(1)} %get-tuple-element.13.mid_ref, bf16[96,512]{1,0:T(8,128)(2,1)S(1)} %get-tuple-element.11.tail_ref), custom_call_target="tpu_custom_call" | custom-call | tf_op jit(solution)/shard_map/pallas_call | solution.py:26
  8.2 0.0 collective-permute-done.lo_ref
  8.2 3.0 %collective-permute-done.1.hi_ref = bf16[96,512]{1,0:T(8,128)(2,1)S(1)} collective-permute-done((bf16[96,512]{1,0:T(8,128)(2,1)S(1)}, bf16[96,512]{1,0:T(8,128)(2,1)S(1)}, u32[]{:S(2)}, u32[]{:S(2)}) %collective-permute-start.1) | collective-permute-done | bytes 98336 | tf_op jit(solution)/shard_map/ppermute | solution.py:218
  11.1 1.3 %shard_map.77 = f32[4,16,8,128]{3,2,1,0:T(8,128)} custom-call(bf16[96,512]{1,0:T(8,128)(2,1)S(1)} %collective-permute-done.lo_ref, bf16[96,512]{1,0:T(8,128)(2,1)S(1)} %get-tuple-element.12.head_ref, bf16[96,512]{1,0:T(8,128)(2,1)S(1)} %get-tuple-element.11.tail_ref, bf16[96,512]{1,0:T(8,128)(2,1)S(1)} %collective-permute-done.1.hi_ref, ...), custom_call_target="tpu_custom_call" | custom-call | tf_op jit(solution)/shard_map/pallas_call | solution.py:26
  12.4 0.0 copy-start
  12.5 16.8 %all-to-all-start = ((f32[64,8,128]{2,1,0:T(8,128)}), f32[64,8,128]{2,1,0:T(8,128)S(1)}, u32[]{:S(2)}, u32[]{:S(2)}) async-start(f32[64,8,128]{2,1,0:T(8,128)} %bitcast.2), calls=%async_computation | async-start | bytes 524288 | tf_op jit(solution)/shard_map/all_to_all | solution.py:206
  29.3 0.0 copy-done
  29.3 0.2 reshape_reshape.3
  29.5 0.1 copy.12
  29.7 0.0 copy-start.2
  29.7 0.6 copy-done.2
  30.3 0.1 copy.13.bias_ref
  30.4 1.7 %shard_map.78 = bf16[64,4,512]{2,1,0:T(4,128)(2,1)} custom-call(bf16[96,512]{1,0:T(8,128)(2,1)S(1)} %collective-permute-done.lo_ref, bf16[96,512]{1,0:T(8,128)(2,1)S(1)} %get-tuple-element.12.head_ref, bf16[2,96,512]{2,1,0:T(8,128)(2,1)S(1)} %get-tuple-element.13.mid_ref, bf16[96,512]{1,0:T(8,128)(2,1)S(1)} %get-tuple-element.11.tail_ref, ...), custom_call_target="tpu_custom_call" | custom-call | tf_op jit(solution)/shard_map/pallas_call | solution.py:26
  32.1 9.6 %all-to-all-done = f32[64,8,128]{2,1,0:T(8,128)S(1)} async-done(((f32[64,8,128]{2,1,0:T(8,128)}), f32[64,8,128]{2,1,0:T(8,128)S(1)}, u32[]{:S(2)}, u32[]{:S(2)}) %all-to-all-start) | async-done | bytes 262176 | tf_op jit(solution)/shard_map/all_to_all | solution.py:206
  41.7 0.1 reduce_sum.18._
  41.8 0.6 broadcast_in_dim.17
  42.4 13.7 %all-to-all-start.1 = ((f32[16,8,128]{2,1,0:T(8,128)}), f32[16,8,128]{2,1,0:T(8,128)S(1)}, u32[]{:S(2)}, u32[]{:S(2)}) async-start(f32[16,8,128]{2,1,0:T(8,128)} %broadcast_in_dim.17), calls=%async_computation.1 | async-start | bytes 131072 | tf_op jit(solution)/shard_map/all_to_all | solution.py:206
  56.1 0.2 reshape.31
  56.3 0.2 copy.14
  56.5 0.2 reshape.33.w_ref
  56.7 1.6 %shard_map.79 = bf16[32,4,512]{2,1,0:T(4,128)(2,1)} custom-call(bf16[96,512]{1,0:T(8,128)(2,1)S(1)} %collective-permute-done.lo_ref, bf16[96,512]{1,0:T(8,128)(2,1)S(1)} %get-tuple-element.12.head_ref, bf16[2,96,512]{2,1,0:T(8,128)(2,1)S(1)} %get-tuple-element.13.mid_ref, bf16[96,512]{1,0:T(8,128)(2,1)S(1)} %get-tuple-element.11.tail_ref, ...), custom_call_target="tpu_custom_call" | custom-call | tf_op jit(solution)/shard_map/pallas_call | solution.py:26
  58.3 9.4 %all-to-all-done.1 = f32[16,8,128]{2,1,0:T(8,128)S(1)} async-done(((f32[16,8,128]{2,1,0:T(8,128)}), f32[16,8,128]{2,1,0:T(8,128)S(1)}, u32[]{:S(2)}, u32[]{:S(2)}) %all-to-all-start.1) | async-done | bytes 65568 | tf_op jit(solution)/shard_map/all_to_all | solution.py:206
  67.7 17.1 %all_to_all.15 = bf16[64,8,128]{2,1,0:T(8,128)(2,1)S(1)} all-to-all(bf16[64,8,128]{2,1,0:T(8,128)(2,1)S(1)} %broadcast_in_dim.19), channel_id=1, replica_groups=mesh['dp_0'=16,'dp_1'=8,'dp_2'=2,'gz'=4] {'dp_1','dp_2','gz'}, dimensions={0} | all-to-all | bytes 262144 | tf_op jit(solution)/shard_map/all_to_all | solution.py:206
  84.8 0.0 copy-start.1
  84.8 0.6 slice_bitcast_fusion
  85.4 0.1 copy-done.1
  (4 shorter events, 0.1 us)
Async XLA Ops:
  1.8 6.3 %collective-permute-start = (bf16[96,512]{1,0:T(8,128)(2,1)S(1)}, bf16[96,512]{1,0:T(8,128)(2,1)S(1)}, u32[]{:S(2)}, u32[]{:S(2)}) collective-permute-start(bf16[96,512]{1,0:T(8,128)(2,1)S(1)} %get-tuple-element.11.tail_ref), channel_id=1, source_target_pairs={{0,1},{1,2},{2,3},{4,5},{5,6},{6,7},{8,9},{9,10},{10,11},{12,13},{... | collective-permute-start | bytes 294920 | tf_op jit(solution)/shard_map/ppermute | solution.py:217
  5.8 5.4 %collective-permute-start.1 = (bf16[96,512]{1,0:T(8,128)(2,1)S(1)}, bf16[96,512]{1,0:T(8,128)(2,1)S(1)}, u32[]{:S(2)}, u32[]{:S(2)}) collective-permute-start(bf16[96,512]{1,0:T(8,128)(2,1)S(1)} %get-tuple-element.12.head_ref), channel_id=1, source_target_pairs={{1,0},{2,1},{3,2},{5,4},{6,5},{7,6},{9,8},{10,9},{11,10},{13,12},{... | collective-permute-start | bytes 294920 | tf_op jit(solution)/shard_map/ppermute | solution.py:218
  12.4 16.8 %copy-start = (bf16[27,2048]{1,0:T(8,128)(2,1)S(1)}, bf16[27,2048]{1,0:T(8,128)(2,1)}, u32[]{:S(2)}) copy-start(bf16[27,2048]{1,0:T(8,128)(2,1)} %param.5) | copy-start | bytes 331780
  12.5 29.2 %all-to-all-start = ((f32[64,8,128]{2,1,0:T(8,128)}), f32[64,8,128]{2,1,0:T(8,128)S(1)}, u32[]{:S(2)}, u32[]{:S(2)}) async-start(f32[64,8,128]{2,1,0:T(8,128)} %bitcast.2), calls=%async_computation | async-start | bytes 524288 | tf_op jit(solution)/shard_map/all_to_all | solution.py:206
  29.7 0.7 copy-start.2
  42.4 25.3 %all-to-all-start.1 = ((f32[16,8,128]{2,1,0:T(8,128)}), f32[16,8,128]{2,1,0:T(8,128)S(1)}, u32[]{:S(2)}, u32[]{:S(2)}) async-start(f32[16,8,128]{2,1,0:T(8,128)} %broadcast_in_dim.17), calls=%async_computation.1 | async-start | bytes 131072 | tf_op jit(solution)/shard_map/all_to_all | solution.py:206
  84.8 0.7 copy-start.1

commit v4 on v3

--- a/solution.py
+++ b/solution.py
@@ -15,6 +15,7 @@
 NEAR = ("dp_1", "dp_2", "gz")
 TILES = 64
 ROWS = 32
+BIAS_ROW = 27
 INTERPRET = False
 VMEM = pl.BlockSpec(memory_space=pltpu.VMEM)
 
@@ -82,7 +83,7 @@
     return lax.dot_general(a, b, dims, preferred_element_type=jnp.float32)
 
 
-def own_body(cin, head_ref, mid_ref, tail_ref, w_ref, s_ref):
+def own_body(cin, head_ref, mid_ref, tail_ref, w_ref, moved_ref, s_ref):
     width = head_ref.shape[1]
     cout = head_ref.shape[0] - cin
     taps = 9 * cin
@@ -91,6 +92,7 @@
     planes = len(own)
     for z in range(planes):
         store_moved(s_ref, z * taps, own[z])
+    moved_ref[...] = s_ref[:taps, :]
     twice = [jnp.concatenate([up, up], axis=0) for up in ups]
     for a in range(3):
         total = jnp.zeros((taps, 2 * cout), jnp.float32)
@@ -104,19 +106,18 @@
     for z in range(planes):
         bias += dot(ones, twice[z], NT)
     w_ref[3 * taps :, :] = jnp.zeros((w_ref.shape[0] - 3 * taps, 2 * cout), jnp.float32)
-    w_ref[3 * taps : 3 * taps + 8, :] = bias[:8]
-
-
-def edge_body(cin, factor, lo_ref, head_ref, tail_ref, hi_ref, w_ref, tiles_ref, s_ref, v_ref):
+    for row in (BIAS_ROW, BIAS_ROW + 1):
+        w_ref[row * cin : row * cin + 8, :] = bias[:8]
+
+
+def edge_body(cin, factor, lo_ref, head_ref, moved_ref, w_ref, tiles_ref, s_ref, v_ref):
     cout = lo_ref.shape[0] - cin
     taps = 9 * cin
     v_ref[...] = w_ref[...]
-    for a, there_ref, here_ref in ((0, lo_ref, head_ref), (2, hi_ref, tail_ref)):
-        at = a // 2 * taps
-        store_moved(s_ref, at, there_ref[:cin, :])
-        up = here_ref[cin:, :]
+    store_moved(s_ref, 0, lo_ref[:cin, :])
+    for a, sources_ref, up in ((0, s_ref, head_ref[cin:, :]), (2, moved_ref, lo_ref[cin:, :])):
         twice = jnp.concatenate([up, up], axis=0)
-        v_ref[a * taps : (a + 1) * taps, :] += dot(s_ref[at : at + taps, :], twice, NT)
+        v_ref[a * taps : (a + 1) * taps, :] += dot(sources_ref[...], twice, NT)
     left = lax.broadcasted_iota(jnp.int32, (ROWS, 2 * cout), 1) < cout
     for at in range(cin // 2):
         even = v_ref[pl.ds(2 * at, ROWS, stride=cin), :]
@@ -166,18 +167,18 @@
     planes = mid.shape[0] + 2
     return on_core(
         functools.partial(own_body, cin),
-        jax.ShapeDtypeStruct((ROWS * cin, 2 * (rows - cin)), jnp.float32),
+        (jax.ShapeDtypeStruct((ROWS * cin, 2 * (rows - cin)), jnp.float32), jax.ShapeDtypeStruct((9 * cin, width), jnp.bfloat16)),
         [pltpu.VMEM((planes * 9 * cin, width), jnp.bfloat16)],
     )(head, mid, tail)
 
 
-def weight_tiles(cin, lo, head, tail, hi, own, factor):
+def weight_tiles(cin, lo, head, head_moved, own, factor):
     rows, width = lo.shape
     return on_core(
         functools.partial(edge_body, cin, factor),
         jax.ShapeDtypeStruct((ROWS // 8, cin // 2, 8, 2 * (rows - cin)), jnp.float32),
-        [pltpu.VMEM((18 * cin, width), jnp.bfloat16), pltpu.VMEM(own.shape, jnp.float32)],
-    )(lo, head, tail, hi, own)
+        [pltpu.VMEM((9 * cin, width), jnp.bfloat16), pltpu.VMEM(own.shape, jnp.float32)],
+    )(lo, head, head_moved, own)
 
 
 def forward(cin, slabs, taps, bias):
@@ -214,24 +215,33 @@
     factor = 1.0 / math.sqrt(cells_all)
     head, mid, tail = split_planes(feats, grads)
     slabs = lax.axis_size("gz")
-    lo = lax.ppermute(tail, "gz", [(i, i + 1) for i in range(slabs - 1)])
-    hi = lax.ppermute(head, "gz", [(i + 1, i) for i in range(slabs - 1)])
+    with jax.named_scope("below"):
+        lo = lax.ppermute(tail, "gz", [(i, i + 1) for i in range(slabs - 1)])
+    own, head_moved = own_terms(cin, head, mid, tail)
+    tiles = weight_tiles(cin, lo, head, head_moved, own, factor).reshape(TILES, 8, 128)
+    tiles, head_late = lax.optimization_barrier((tiles, head))
+    with jax.named_scope("gather_parts"):
+        parts = swap(tiles, NEAR)
+    with jax.named_scope("above"):
+        hi = lax.ppermute(head_late, "gz", [(i + 1, i) for i in range(slabs - 1)])
     planes = (lo, head, mid, tail, hi)
     kernel = kernel_taps.reshape(27, cin, cout)
     ahead = kernel.reshape(27 * cin, cout).T
     back = kernel[::-1].reshape(3, 9, cin, cout).transpose(1, 2, 0, 3).reshape(9 * cin, 3 * cout)
-    own = own_terms(cin, head, mid, tail)
-    tiles = weight_tiles(cin, lo, head, tail, hi, own, factor).reshape(TILES, 8, 128)
-    part = jnp.sum(swap(tiles, NEAR), axis=0)
     output = forward(cin, planes, ahead, channel_bias[:, None])
-    part, output = lax.optimization_barrier((part, output))
+    part, output = lax.optimization_barrier((jnp.sum(parts, axis=0), output))
     grad_input = backward(cin, planes, back, part)
     far = lax.axis_size("dp_0")
     part = jnp.sum(swap(jnp.broadcast_to(part, (far, *part.shape)), "dp_0"), axis=0)
     part, grad_input = lax.optimization_barrier((part, grad_input))
-    total = swap(jnp.broadcast_to(part.astype(jnp.bfloat16), tiles.shape), NEAR).astype(jnp.float32)
+    rounded = lax.reduce_precision(part, 8, 7)
+    last = lax.axis_index(NEAR) >= TILES - TILES * 8 // ROWS
+    rest = last & (lax.broadcasted_iota(jnp.int32, part.shape, 0) == (BIAS_ROW + 1) % 8)
+    part = jnp.where(rest, part - rounded, rounded).astype(jnp.bfloat16)
+    total = swap(jnp.broadcast_to(part, tiles.shape), NEAR).astype(jnp.float32)
     total = total.reshape(4, 16, 8, 128).transpose(0, 2, 1, 3).reshape(ROWS, 2048)
-    return (output[None], grad_input[None], total[:27], total[27, :cout])
+    bias_total = total[BIAS_ROW, :cout] + total[BIAS_ROW + 1, :cout]
+    return (output[None], grad_input[None], total[:27], bias_total)
 
 
 def solution(mesh):

time: 85.9 us -> 84.7 us (0.986)
  waiting for transfers between devices: 22 us -> 18.1 us
  blocking collectives: 17.1 us -> 19 us
    all_to_all x2, waiting for transfers between devices: 19 us -> 13 us  [swap(): return lax.all_to_all(blocks, axes, 0, 0, tiled=True)]
    all_to_all x1, blocking collectives: 17.1 us -> 19 us  [swap(): return lax.all_to_all(blocks, axes, 0, 0, tiled=True)]
    ppermute x1, waiting for transfers between devices: 2.98 us -> 4.51 us  [on_device(): hi = lax.ppermute(head_late, 'gz', [(i + 1, i) for i in range(slabs - 1)])]
  transfers between devices with their start and end apart: 4 -> 4, of which waited for: 3 -> 4; matrix products, arithmetic and copies ran while one was open for 1% -> 1% of each run, Pallas kernels for 5% -> 5%
where the time goes in v4:
time: 84.7 us; the launch traced here: 84.4 us
  starting transfers between devices  36.5 us (43%)
  blocking collectives  19 us (22%)
  waiting for transfers between devices  18.1 us (21%)
  Pallas kernels  6.84 us (8%)
  local copies, waits for them, and re-layouts  2.47 us (3%)
    all_to_all x2, starting transfers between devices, swap(): return lax.all_to_all(blocks, axes, 0, 0, tiled=True)  31.3 us
    all_to_all x1, blocking collectives, swap(): return lax.all_to_all(blocks, axes, 0, 0, tiled=True)  19 us
    all_to_all x2, waiting for transfers between devices, swap(): return lax.all_to_all(blocks, axes, 0, 0, tiled=True)  13 us
    pallas_call x5, Pallas kernels, call(): pl.pallas_call(body, out_shape=jax.tree.map(lambda s: pltpu.VMEM(s.shape,...  6.84 us
    ppermute x1, waiting for transfers between devices, on_device(): hi = lax.ppermute(head_late, 'gz', [(i + 1, i) for i in range(slabs - 1)])  4.51 us
    ppermute x1, starting transfers between devices, on_device(): lo = lax.ppermute(tail, 'gz', [(i, i + 1) for i in range(slabs - 1)])  3.94 us
  transfers between devices with their start and end apart: 4, of which 4 were waited for; matrix products, arithmetic and copies ran while one was open for 1% of the time, Pallas kernels for 5%

profile of v4, /device:TPU:1, one launch (start us, length us, event | category | flops | bytes accessed | tf_op | source)
XLA Modules:
  0.0 84.4 jit_solution(15884468314947304672)
XLA Ops:
  0.6 1.2 %shard_map.75 = (bf16[96,512]{1,0:T(8,128)(2,1)S(1)}, bf16[2,96,512]{2,1,0:T(8,128)(2,1)S(1)}, bf16[96,512]{1,0:T(8,128)(2,1)S(1)}) custom-call(bf16[32,4,512]{2,1,0:T(4,128)(2,1)} %bitcast.25, bf16[64,4,512]{2,1,0:T(4,128)(2,1)} %bitcast.22), custom_call_target="tpu_custom_call" | custom-call | tf_op jit(solution)/shard_map/pallas_call | solution.py:27
  1.8 3.9 %collective-permute-start = (bf16[96,512]{1,0:T(8,128)(2,1)S(1)}, bf16[96,512]{1,0:T(8,128)(2,1)S(1)}, u32[]{:S(2)}, u32[]{:S(2)}) collective-permute-start(bf16[96,512]{1,0:T(8,128)(2,1)S(1)} %get-tuple-element.15.tail_ref), channel_id=1, source_target_pairs={{0,1},{1,2},{2,3},{4,5},{5,6},{6,7},{8,9},{9,10},{10,11},{12,13},{... | collective-permute-start | bytes 294920 | tf_op jit(solution)/shard_map/below/ppermute | solution.py:219
  5.8 1.1 %shard_map.76 = (f32[1024,128]{1,0:T(8,128)S(1)}, bf16[288,512]{1,0:T(8,128)(2,1)S(1)}) custom-call(bf16[96,512]{1,0:T(8,128)(2,1)S(1)} %get-tuple-element.21.head_ref, bf16[2,96,512]{2,1,0:T(8,128)(2,1)S(1)} %get-tuple-element.17.mid_ref, bf16[96,512]{1,0:T(8,128)(2,1)S(1)} %get-tuple-element.15.tail_ref), custom_call_target="tpu_custom_call" | custom-call | tf_op jit(solution)/shard_map/pallas_call | solution.py:27
  6.9 0.5 collective-permute-done.lo_ref
  7.4 1.3 %shard_map.77 = f32[4,16,8,128]{3,2,1,0:T(8,128)} custom-call(bf16[96,512]{1,0:T(8,128)(2,1)S(1)} %collective-permute-done.lo_ref, bf16[96,512]{1,0:T(8,128)(2,1)S(1)} %get-tuple-element.21.head_ref, bf16[288,512]{1,0:T(8,128)(2,1)S(1)} %get-tuple-element.18.moved_ref, f32[1024,128]{1,0:T(8,128)S(1)} %get-tuple-element.19.w_ref), custom_call_target="tpu_custom_call" | custom-call | tf_op jit(solution)/shard_map/pallas_call | solution.py:27
  8.7 0.0 copy-start
  8.7 16.4 %all-to-all-start = ((f32[64,8,128]{2,1,0:T(8,128)}), f32[64,8,128]{2,1,0:T(8,128)S(1)}, u32[]{:S(2)}, u32[]{:S(2)}) async-start(f32[64,8,128]{2,1,0:T(8,128)} %bitcast.2), calls=%async_computation | async-start | bytes 524288 | tf_op jit(solution)/shard_map/gather_parts/all_to_all | solution.py:207
  25.1 1.3 %collective-permute-start.1 = (bf16[96,512]{1,0:T(8,128)(2,1)S(1)}, bf16[96,512]{1,0:T(8,128)(2,1)S(1)}, u32[]{:S(2)}, u32[]{:S(2)}) collective-permute-start(bf16[96,512]{1,0:T(8,128)(2,1)S(1)} %get-tuple-element.21.head_ref), channel_id=1, source_target_pairs={{1,0},{2,1},{3,2},{5,4},{6,5},{7,6},{9,8},{10,9},{11,10},{13,12},{... | collective-permute-start | bytes 294920 | tf_op jit(solution)/shard_map/above/ppermute | solution.py:226
  26.4 0.0 copy-done
  26.4 0.2 reshape_reshape.3
  26.6 0.1 copy.12
  26.8 0.0 copy-start.2
  26.8 0.6 copy-done.2
  27.4 0.1 copy.13.bias_ref
  27.5 4.5 %collective-permute-done.1.hi_ref = bf16[96,512]{1,0:T(8,128)(2,1)S(1)} collective-permute-done((bf16[96,512]{1,0:T(8,128)(2,1)S(1)}, bf16[96,512]{1,0:T(8,128)(2,1)S(1)}, u32[]{:S(2)}, u32[]{:S(2)}) %collective-permute-start.1) | collective-permute-done | bytes 98336 | tf_op jit(solution)/shard_map/above/ppermute | solution.py:226
  32.0 1.7 %shard_map.78 = bf16[64,4,512]{2,1,0:T(4,128)(2,1)} custom-call(bf16[96,512]{1,0:T(8,128)(2,1)S(1)} %collective-permute-done.lo_ref, bf16[96,512]{1,0:T(8,128)(2,1)S(1)} %get-tuple-element.21.head_ref, bf16[2,96,512]{2,1,0:T(8,128)(2,1)S(1)} %get-tuple-element.17.mid_ref, bf16[96,512]{1,0:T(8,128)(2,1)S(1)} %get-tuple-element.15.tail_ref, ...), custom_call_target="tpu_custom_call" | custom-call | tf_op jit(solution)/shard_map/pallas_call | solution.py:27
  33.7 3.6 %all-to-all-done = f32[64,8,128]{2,1,0:T(8,128)S(1)} async-done(((f32[64,8,128]{2,1,0:T(8,128)}), f32[64,8,128]{2,1,0:T(8,128)S(1)}, u32[]{:S(2)}, u32[]{:S(2)}) %all-to-all-start) | async-done | bytes 262176 | tf_op jit(solution)/shard_map/gather_parts/all_to_all | solution.py:207
  37.4 0.1 reduce_sum.18._
  37.5 0.6 broadcast_in_dim.17
  38.1 14.9 %all-to-all-start.1 = ((f32[16,8,128]{2,1,0:T(8,128)}), f32[16,8,128]{2,1,0:T(8,128)S(1)}, u32[]{:S(2)}, u32[]{:S(2)}) async-start(f32[16,8,128]{2,1,0:T(8,128)} %broadcast_in_dim.17), calls=%async_computation.1 | async-start | bytes 131072 | tf_op jit(solution)/shard_map/all_to_all | solution.py:207
  53.0 0.2 reshape.32
  53.2 0.2 copy.14
  53.4 0.2 reshape.34.w_ref
  53.6 1.6 %shard_map.79 = bf16[32,4,512]{2,1,0:T(4,128)(2,1)} custom-call(bf16[96,512]{1,0:T(8,128)(2,1)S(1)} %collective-permute-done.lo_ref, bf16[96,512]{1,0:T(8,128)(2,1)S(1)} %get-tuple-element.21.head_ref, bf16[2,96,512]{2,1,0:T(8,128)(2,1)S(1)} %get-tuple-element.17.mid_ref, bf16[96,512]{1,0:T(8,128)(2,1)S(1)} %get-tuple-element.15.tail_ref, ...), custom_call_target="tpu_custom_call" | custom-call | tf_op jit(solution)/shard_map/pallas_call | solution.py:27
  55.1 9.4 %all-to-all-done.1 = f32[16,8,128]{2,1,0:T(8,128)S(1)} async-done(((f32[16,8,128]{2,1,0:T(8,128)}), f32[16,8,128]{2,1,0:T(8,128)S(1)}, u32[]{:S(2)}, u32[]{:S(2)}) %all-to-all-start.1) | async-done | bytes 65568 | tf_op jit(solution)/shard_map/all_to_all | solution.py:207
  64.5 0.1 fusion
  64.6 19.0 %all_to_all.15 = bf16[64,8,128]{2,1,0:T(8,128)(2,1)S(1)} all-to-all(bf16[64,8,128]{2,1,0:T(8,128)(2,1)S(1)} %broadcast_in_dim.19), channel_id=1, replica_groups=mesh['dp_0'=16,'dp_1'=8,'dp_2'=2,'gz'=4] {'dp_1','dp_2','gz'}, dimensions={0} | all-to-all | bytes 262144 | tf_op jit(solution)/shard_map/all_to_all | solution.py:207
  83.7 0.0 copy-start.1
  83.7 0.6 fusion.1
  84.2 0.1 copy-done.1
  (5 shorter events, 0.1 us)
Async XLA Ops:
  1.8 5.6 %collective-permute-start = (bf16[96,512]{1,0:T(8,128)(2,1)S(1)}, bf16[96,512]{1,0:T(8,128)(2,1)S(1)}, u32[]{:S(2)}, u32[]{:S(2)}) collective-permute-start(bf16[96,512]{1,0:T(8,128)(2,1)S(1)} %get-tuple-element.15.tail_ref), channel_id=1, source_target_pairs={{0,1},{1,2},{2,3},{4,5},{5,6},{6,7},{8,9},{9,10},{10,11},{12,13},{... | collective-permute-start | bytes 294920 | tf_op jit(solution)/shard_map/below/ppermute | solution.py:219
  8.7 17.7 %copy-start = (bf16[27,2048]{1,0:T(8,128)(2,1)S(1)}, bf16[27,2048]{1,0:T(8,128)(2,1)}, u32[]{:S(2)}) copy-start(bf16[27,2048]{1,0:T(8,128)(2,1)} %param.5) | copy-start | bytes 331780
  8.7 28.7 %all-to-all-start = ((f32[64,8,128]{2,1,0:T(8,128)}), f32[64,8,128]{2,1,0:T(8,128)S(1)}, u32[]{:S(2)}, u32[]{:S(2)}) async-start(f32[64,8,128]{2,1,0:T(8,128)} %bitcast.2), calls=%async_computation | async-start | bytes 524288 | tf_op jit(solution)/shard_map/gather_parts/all_to_all | solution.py:207
  25.1 6.9 %collective-permute-start.1 = (bf16[96,512]{1,0:T(8,128)(2,1)S(1)}, bf16[96,512]{1,0:T(8,128)(2,1)S(1)}, u32[]{:S(2)}, u32[]{:S(2)}) collective-permute-start(bf16[96,512]{1,0:T(8,128)(2,1)S(1)} %get-tuple-element.21.head_ref), channel_id=1, source_target_pairs={{1,0},{2,1},{3,2},{5,4},{6,5},{7,6},{9,8},{10,9},{11,10},{13,12},{... | collective-permute-start | bytes 294920 | tf_op jit(solution)/shard_map/above/ppermute | solution.py:226
  26.8 0.7 copy-start.2
  38.1 26.4 %all-to-all-start.1 = ((f32[16,8,128]{2,1,0:T(8,128)}), f32[16,8,128]{2,1,0:T(8,128)S(1)}, u32[]{:S(2)}, u32[]{:S(2)}) async-start(f32[16,8,128]{2,1,0:T(8,128)} %broadcast_in_dim.17), calls=%async_computation.1 | async-start | bytes 131072 | tf_op jit(solution)/shard_map/all_to_all | solution.py:207
  83.7 0.7 copy-start.1

commit v5 on v4

--- a/solution.py
+++ b/solution.py
@@ -12,22 +12,24 @@
 NX = 64
 NY = 8
 DP = ("dp_0", "dp_1", "dp_2")
-NEAR = ("dp_1", "dp_2", "gz")
-TILES = 64
+CORE = "dp_2"
+NEAR = ("dp_1", "gz")
+TILES = 32
 ROWS = 32
 BIAS_ROW = 27
 INTERPRET = False
 VMEM = pl.BlockSpec(memory_space=pltpu.VMEM)
+SMEM = pl.BlockSpec(memory_space=pltpu.SMEM)
 
 
 def on_core(body, out_shape, scratch=(), held=True, near=True):
     def call(*operands):
         if held:
-            operands = [pltpu.with_memory_space_constraint(x, pltpu.VMEM) for x in operands]
+            operands = [x if x.ndim == 1 else pltpu.with_memory_space_constraint(x, pltpu.VMEM) for x in operands]
         return pl.pallas_call(
             body,
             out_shape=jax.tree.map(lambda s: pltpu.VMEM(s.shape, s.dtype), out_shape) if near else out_shape,
-            in_specs=[VMEM] * len(operands),
+            in_specs=[SMEM if x.ndim == 1 else VMEM for x in operands],
             out_specs=jax.tree.map(lambda _: VMEM, out_shape),
             scratch_shapes=list(scratch),
             interpret=INTERPRET,
@@ -110,7 +112,7 @@
         w_ref[row * cin : row * cin + 8, :] = bias[:8]
 
 
-def edge_body(cin, factor, lo_ref, head_ref, moved_ref, w_ref, tiles_ref, s_ref, v_ref):
+def edge_body(cin, factor, core_ref, lo_ref, head_ref, moved_ref, w_ref, keep_ref, send_ref, s_ref, v_ref):
     cout = lo_ref.shape[0] - cin
     taps = 9 * cin
     v_ref[...] = w_ref[...]
@@ -119,13 +121,16 @@
         twice = jnp.concatenate([up, up], axis=0)
         v_ref[a * taps : (a + 1) * taps, :] += dot(sources_ref[...], twice, NT)
     left = lax.broadcasted_iota(jnp.int32, (ROWS, 2 * cout), 1) < cout
+    first = core_ref[0] == 0
     for at in range(cin // 2):
         even = v_ref[pl.ds(2 * at, ROWS, stride=cin), :]
         odd = v_ref[pl.ds(2 * at + 1, ROWS, stride=cin), :]
-        tiles_ref[:, at] = (jnp.where(left, even, odd) * factor).reshape(ROWS // 8, 8, 2 * cout)
-
-
-def forward_body(cin, lo_ref, head_ref, mid_ref, tail_ref, hi_ref, w_ref, bias_ref, out_ref, s_ref):
+        both = (jnp.where(left, even, odd) * factor).reshape(2, ROWS // 16, 8, 2 * cout)
+        keep_ref[:, at] = jnp.where(first, both[0], both[1])
+        send_ref[:, at] = jnp.where(first, both[1], both[0])
+
+
+def forward_body(cin, lo_ref, head_ref, mid_ref, tail_ref, hi_ref, w_ref, bias_ref, _, out_ref, s_ref):
     taps = 9 * cin
     rows = slice(0, cin)
     slabs = [lo_ref[rows, :], *planes_of(head_ref, mid_ref, tail_ref, rows), hi_ref[rows, :]]
@@ -172,16 +177,17 @@
     )(head, mid, tail)
 
 
-def weight_tiles(cin, lo, head, head_moved, own, factor):
+def weight_tiles(cin, core, lo, head, head_moved, own, factor):
     rows, width = lo.shape
+    half = jax.ShapeDtypeStruct((ROWS // 16, cin // 2, 8, 2 * (rows - cin)), jnp.float32)
     return on_core(
         functools.partial(edge_body, cin, factor),
-        jax.ShapeDtypeStruct((ROWS // 8, cin // 2, 8, 2 * (rows - cin)), jnp.float32),
+        (half, half),
         [pltpu.VMEM((9 * cin, width), jnp.bfloat16), pltpu.VMEM(own.shape, jnp.float32)],
-    )(lo, head, head_moved, own)
-
-
-def forward(cin, slabs, taps, bias):
+    )(core, lo, head, head_moved, own)
+
+
+def forward(cin, slabs, taps, bias, after):
     rows, width = slabs[0].shape
     planes = slabs[2].shape[0] + 2
     return on_core(
@@ -189,7 +195,7 @@
         jax.ShapeDtypeStruct((rows - cin, planes, width), jnp.bfloat16),
         [pltpu.VMEM(((planes + 2) * 9 * cin, width), jnp.bfloat16)],
         near=False,
-    )(*slabs, taps, bias)
+    )(*slabs, taps, bias, after)
 
 
 def backward(cin, slabs, taps, after):
@@ -218,27 +224,28 @@
     with jax.named_scope("below"):
         lo = lax.ppermute(tail, "gz", [(i, i + 1) for i in range(slabs - 1)])
     own, head_moved = own_terms(cin, head, mid, tail)
-    tiles = weight_tiles(cin, lo, head, head_moved, own, factor).reshape(TILES, 8, 128)
+    core = lax.axis_index(CORE)
+    keep, send = weight_tiles(cin, core[None], lo, head, head_moved, own, factor)
+    tiles = (keep + lax.ppermute(send, CORE, [(0, 1), (1, 0)])).reshape(TILES, 8, 128)
     tiles, head_late = lax.optimization_barrier((tiles, head))
-    with jax.named_scope("gather_parts"):
-        parts = swap(tiles, NEAR)
-    with jax.named_scope("above"):
-        hi = lax.ppermute(head_late, "gz", [(i + 1, i) for i in range(slabs - 1)])
-    planes = (lo, head, mid, tail, hi)
+    parts = swap(tiles, NEAR)
+    hi = lax.ppermute(head_late, "gz", [(i + 1, i) for i in range(slabs - 1)])
     kernel = kernel_taps.reshape(27, cin, cout)
     ahead = kernel.reshape(27 * cin, cout).T
     back = kernel[::-1].reshape(3, 9, cin, cout).transpose(1, 2, 0, 3).reshape(9 * cin, 3 * cout)
-    output = forward(cin, planes, ahead, channel_bias[:, None])
-    part, output = lax.optimization_barrier((jnp.sum(parts, axis=0), output))
+    bias = channel_bias[:, None]
+    part, hi, ahead, back, bias = lax.optimization_barrier((jnp.sum(parts, axis=0), hi, ahead, back, bias))
+    planes = (lo, head, mid, tail, hi)
+    output = forward(cin, planes, ahead, bias, part)
     grad_input = backward(cin, planes, back, part)
     far = lax.axis_size("dp_0")
     part = jnp.sum(swap(jnp.broadcast_to(part, (far, *part.shape)), "dp_0"), axis=0)
-    part, grad_input = lax.optimization_barrier((part, grad_input))
+    part, output, grad_input = lax.optimization_barrier((part, output, grad_input))
     rounded = lax.reduce_precision(part, 8, 7)
-    last = lax.axis_index(NEAR) >= TILES - TILES * 8 // ROWS
+    last = core * TILES + lax.axis_index(NEAR) >= BIAS_ROW // 8 * (cin // 2)
     rest = last & (lax.broadcasted_iota(jnp.int32, part.shape, 0) == (BIAS_ROW + 1) % 8)
     part = jnp.where(rest, part - rounded, rounded).astype(jnp.bfloat16)
-    total = swap(jnp.broadcast_to(part, tiles.shape), NEAR).astype(jnp.float32)
+    total = lax.all_gather(swap(jnp.broadcast_to(part, tiles.shape), NEAR), CORE).astype(jnp.float32)
     total = total.reshape(4, 16, 8, 128).transpose(0, 2, 1, 3).reshape(ROWS, 2048)
     bias_total = total[BIAS_ROW, :cout] + total[BIAS_ROW + 1, :cout]
     return (output[None], grad_input[None], total[:27], bias_total)

time: 84.7 us -> 85.6 us (1.011)
  waiting for transfers between devices: 18.1 us -> 16.3 us
  starting transfers between devices: 36.5 us -> 37.9 us
  blocking collectives: 19 us -> 20.2 us
    ppermute x0 -> x1, starting transfers between devices: none -> 14 us  [on_device(): lax.ppermute(send, CORE, [(0, 1), (1, 0)])]
    all_to_all x2, starting transfers between devices: 31.3 us -> 18.7 us  [swap(): return lax.all_to_all(blocks, axes, 0, 0, tiled=True)]
    all_gather x0 -> x1, blocking collectives: none -> 6.34 us  [on_device(): lax.all_gather(swap(jnp.broadcast_to(part, tiles.shape), NEAR), CORE)]
    all_to_all x1, blocking collectives: 19 us -> 13.9 us  [swap(): return lax.all_to_all(blocks, axes, 0, 0, tiled=True)]
    ppermute x1, waiting for transfers between devices: 4.51 us -> 0.01 us  [on_device(): hi = lax.ppermute(head_late, 'gz', [(i + 1, i) for i in range(slabs - 1)])]
    all_to_all x2, waiting for transfers between devices: 13 us -> 14.8 us  [swap(): return lax.all_to_all(blocks, axes, 0, 0, tiled=True)]
    ppermute x0 -> x1, waiting for transfers between devices: none -> 0.96 us  [on_device(): lax.ppermute(send, CORE, [(0, 1), (1, 0)])]
  transfers between devices with their start and end apart: 4 -> 5, of which waited for: 4 -> 4; matrix products, arithmetic and copies ran while one was open for 1% -> 1% of each run, Pallas kernels for 5% -> 5%
where the time goes in v5:
time: 85.6 us; the launch traced here: 85.2 us
  starting transfers between devices  37.9 us (44%)
  blocking collectives  20.2 us (24%)
  waiting for transfers between devices  16.3 us (19%)
  Pallas kernels  6.16 us (7%)
  local copies, waits for them, and re-layouts  2.45 us (3%)
  other arithmetic  1.38 us (2%)
    all_to_all x2, starting transfers between devices, swap(): return lax.all_to_all(blocks, axes, 0, 0, tiled=True)  18.7 us
    all_to_all x2, waiting for transfers between devices, swap(): return lax.all_to_all(blocks, axes, 0, 0, tiled=True)  14.8 us
    ppermute x1, starting transfers between devices, on_device(): lax.ppermute(send, CORE, [(0, 1), (1, 0)])  14 us
    all_to_all x1, blocking collectives, swap(): return lax.all_to_all(blocks, axes, 0, 0, tiled=True)  13.9 us
    all_gather x1, blocking collectives, on_device(): lax.all_gather(swap(jnp.broadcast_to(part, tiles.shape), NEAR), CORE)  6.34 us
    pallas_call x5, Pallas kernels, call(): pl.pallas_call(body, out_shape=jax.tree.map(lambda s: pltpu.VMEM(s.shape,...  6.16 us
    ppermute x1, starting transfers between devices, on_device(): lo = lax.ppermute(tail, 'gz', [(i, i + 1) for i in range(slabs - 1)])  3.94 us
  transfers between devices with their start and end apart: 5, of which 4 were waited for; matrix products, arithmetic and copies ran while one was open for 1% of the time, Pallas kernels for 5%

profile of v5, /device:TPU:1, one launch (start us, length us, event | category | flops | bytes accessed | tf_op | source)
XLA Modules:
  0.0 85.2 jit_solution(1827174716107990640)
XLA Ops:
  0.6 1.2 %shard_map.75 = (bf16[96,512]{1,0:T(8,128)(2,1)S(1)}, bf16[2,96,512]{2,1,0:T(8,128)(2,1)S(1)}, bf16[96,512]{1,0:T(8,128)(2,1)S(1)}) custom-call(bf16[32,4,512]{2,1,0:T(4,128)(2,1)} %bitcast.26, bf16[64,4,512]{2,1,0:T(4,128)(2,1)} %bitcast.23), custom_call_target="tpu_custom_call" | custom-call | tf_op jit(solution)/shard_map/pallas_call | solution.py:29
  1.8 3.9 %collective-permute-start = (bf16[96,512]{1,0:T(8,128)(2,1)S(1)}, bf16[96,512]{1,0:T(8,128)(2,1)S(1)}, u32[]{:S(2)}, u32[]{:S(2)}) collective-permute-start(bf16[96,512]{1,0:T(8,128)(2,1)S(1)} %get-tuple-element.21.tail_ref), channel_id=1, source_target_pairs={{0,1},{1,2},{2,3},{4,5},{5,6},{6,7},{8,9},{9,10},{10,11},{12,13},{... | collective-permute-start | bytes 294920 | tf_op jit(solution)/shard_map/below/ppermute | solution.py:225
  5.8 1.1 %shard_map.76 = (f32[1024,128]{1,0:T(8,128)S(1)}, bf16[288,512]{1,0:T(8,128)(2,1)S(1)}) custom-call(bf16[96,512]{1,0:T(8,128)(2,1)S(1)} %get-tuple-element.29.head_ref, bf16[2,96,512]{2,1,0:T(8,128)(2,1)S(1)} %get-tuple-element.23.mid_ref, bf16[96,512]{1,0:T(8,128)(2,1)S(1)} %get-tuple-element.21.tail_ref), custom_call_target="tpu_custom_call" | custom-call | tf_op jit(solution)/shard_map/pallas_call | solution.py:29
  6.9 0.5 collective-permute-done.lo_ref
  7.4 0.6 shard_map.77
  8.0 14.0 %collective-permute-start.1 = (f32[2,16,8,128]{3,2,1,0:T(8,128)S(1)}, f32[2,16,8,128]{3,2,1,0:T(8,128)S(1)}, u32[]{:S(2)}, u32[]{:S(2)}) collective-permute-start(f32[2,16,8,128]{3,2,1,0:T(8,128)S(1)} %get-tuple-element.27), channel_id=1, source_target_pairs={{0,4},{4,0},{1,5},{5,1},{2,6},{6,2},{3,7},{7,3},{8,12},{12,8},{9,1... | collective-permute-start | bytes 393224 | tf_op jit(solution)/shard_map/ppermute | solution.py:229
  22.0 1.0 %collective-permute-done.1 = f32[2,16,8,128]{3,2,1,0:T(8,128)S(1)} collective-permute-done((f32[2,16,8,128]{3,2,1,0:T(8,128)S(1)}, f32[2,16,8,128]{3,2,1,0:T(8,128)S(1)}, u32[]{:S(2)}, u32[]{:S(2)}) %collective-permute-start.1) | collective-permute-done | bytes 131104 | tf_op jit(solution)/shard_map/ppermute | solution.py:229
  22.9 0.7 add.15
  23.6 0.0 copy-start
  23.6 4.0 %all-to-all-start = ((f32[32,8,128]{2,1,0:T(8,128)}), f32[32,8,128]{2,1,0:T(8,128)S(1)}, u32[]{:S(2)}, u32[]{:S(2)}) async-start(f32[32,8,128]{2,1,0:T(8,128)} %bitcast.3), calls=%async_computation | async-start | bytes 262144 | tf_op jit(solution)/shard_map/all_to_all | solution.py:213
  27.6 1.3 %collective-permute-start.2 = (bf16[96,512]{1,0:T(8,128)(2,1)S(1)}, bf16[96,512]{1,0:T(8,128)(2,1)S(1)}, u32[]{:S(2)}, u32[]{:S(2)}) collective-permute-start(bf16[96,512]{1,0:T(8,128)(2,1)S(1)} %get-tuple-element.29.head_ref), channel_id=1, source_target_pairs={{1,0},{2,1},{3,2},{5,4},{6,5},{7,6},{9,8},{10,9},{11,10},{13,12},{... | collective-permute-start | bytes 294920 | tf_op jit(solution)/shard_map/ppermute | solution.py:232
  28.9 0.0 copy-done
  28.9 0.2 reshape.32
  29.1 0.2 reshape_reshape.3
  29.4 0.2 copy.16
  29.5 0.2 reshape.34.w_ref
  29.7 0.1 copy.15
  29.9 7.2 %all-to-all-done = f32[32,8,128]{2,1,0:T(8,128)S(1)} async-done(((f32[32,8,128]{2,1,0:T(8,128)}), f32[32,8,128]{2,1,0:T(8,128)S(1)}, u32[]{:S(2)}, u32[]{:S(2)}) %all-to-all-start) | async-done | bytes 131104 | tf_op jit(solution)/shard_map/all_to_all | solution.py:213
  37.1 0.0 collective-permute-done.2.hi_ref
  37.1 0.6 broadcast_in_dim.20
  37.7 14.7 %all-to-all-start.1 = ((f32[16,8,128]{2,1,0:T(8,128)}), f32[16,8,128]{2,1,0:T(8,128)S(1)}, u32[]{:S(2)}, u32[]{:S(2)}) async-start(f32[16,8,128]{2,1,0:T(8,128)} %broadcast_in_dim.20), calls=%async_computation.1 | async-start | bytes 131072 | tf_op jit(solution)/shard_map/all_to_all | solution.py:213
  52.4 0.0 copy-start.2
  52.5 0.6 copy-done.2
  53.1 0.1 copy.17.bias_ref
  53.2 1.6 %shard_map.79 = bf16[32,4,512]{2,1,0:T(4,128)(2,1)} custom-call(bf16[96,512]{1,0:T(8,128)(2,1)S(1)} %collective-permute-done.lo_ref, bf16[96,512]{1,0:T(8,128)(2,1)S(1)} %get-tuple-element.29.head_ref, bf16[2,96,512]{2,1,0:T(8,128)(2,1)S(1)} %get-tuple-element.23.mid_ref, bf16[96,512]{1,0:T(8,128)(2,1)S(1)} %get-tuple-element.21.tail_ref, ...), custom_call_target="tpu_custom_call" | custom-call | tf_op jit(solution)/shard_map/pallas_call | solution.py:29
  54.8 1.7 %shard_map.78 = bf16[64,4,512]{2,1,0:T(4,128)(2,1)} custom-call(bf16[96,512]{1,0:T(8,128)(2,1)S(1)} %collective-permute-done.lo_ref, bf16[96,512]{1,0:T(8,128)(2,1)S(1)} %get-tuple-element.29.head_ref, bf16[2,96,512]{2,1,0:T(8,128)(2,1)S(1)} %get-tuple-element.23.mid_ref, bf16[96,512]{1,0:T(8,128)(2,1)S(1)} %get-tuple-element.21.tail_ref, ...), custom_call_target="tpu_custom_call" | custom-call | tf_op jit(solution)/shard_map/pallas_call | solution.py:29
  56.5 7.6 %all-to-all-done.1 = f32[16,8,128]{2,1,0:T(8,128)S(1)} async-done(((f32[16,8,128]{2,1,0:T(8,128)}), f32[16,8,128]{2,1,0:T(8,128)S(1)}, u32[]{:S(2)}, u32[]{:S(2)}) %all-to-all-start.1) | async-done | bytes 65568 | tf_op jit(solution)/shard_map/all_to_all | solution.py:213
  64.1 0.1 fusion
  64.2 13.9 %all_to_all.15 = bf16[32,8,128]{2,1,0:T(8,128)(2,1)S(1)} all-to-all(bf16[32,8,128]{2,1,0:T(8,128)(2,1)S(1)} %broadcast_in_dim.23), channel_id=1, replica_groups=mesh['dp_0'=16,'dp_1'=8,'dp_2'=2,'gz'=4] {'dp_1','gz'}, dimensions={0} | all-to-all | bytes 131072 | tf_op jit(solution)/shard_map/all_to_all | solution.py:213
  78.1 6.3 %all-gather = bf16[64,8,128]{2,1,0:T(8,128)(2,1)S(1)} all-gather(bf16[32,8,128]{2,1,0:T(8,128)(2,1)S(1)} %all_to_all.15), channel_id=2, replica_groups=mesh['dp_0'=16,'dp_1'=8,'dp_2'=2,'gz'=4] {'dp_2'}, dimensions={0}, use_global_device_ids=true | all-gather | bytes 196608 | tf_op jit(solution)/shard_map/all_gather | solution.py:248
  84.5 0.0 copy-start.1
  84.5 0.6 fusion.1
  85.0 0.1 copy-done.1
  (6 shorter events, 0.1 us)
Async XLA Ops:
  1.8 5.6 %collective-permute-start = (bf16[96,512]{1,0:T(8,128)(2,1)S(1)}, bf16[96,512]{1,0:T(8,128)(2,1)S(1)}, u32[]{:S(2)}, u32[]{:S(2)}) collective-permute-start(bf16[96,512]{1,0:T(8,128)(2,1)S(1)} %get-tuple-element.21.tail_ref), channel_id=1, source_target_pairs={{0,1},{1,2},{2,3},{4,5},{5,6},{6,7},{8,9},{9,10},{10,11},{12,13},{... | collective-permute-start | bytes 294920 | tf_op jit(solution)/shard_map/below/ppermute | solution.py:225
  8.0 14.9 %collective-permute-start.1 = (f32[2,16,8,128]{3,2,1,0:T(8,128)S(1)}, f32[2,16,8,128]{3,2,1,0:T(8,128)S(1)}, u32[]{:S(2)}, u32[]{:S(2)}) collective-permute-start(f32[2,16,8,128]{3,2,1,0:T(8,128)S(1)} %get-tuple-element.27), channel_id=1, source_target_pairs={{0,4},{4,0},{1,5},{5,1},{2,6},{6,2},{3,7},{7,3},{8,12},{12,8},{9,1... | collective-permute-start | bytes 393224 | tf_op jit(solution)/shard_map/ppermute | solution.py:229
  23.6 5.3 %copy-start = (bf16[27,2048]{1,0:T(8,128)(2,1)S(1)}, bf16[27,2048]{1,0:T(8,128)(2,1)}, u32[]{:S(2)}) copy-start(bf16[27,2048]{1,0:T(8,128)(2,1)} %param.5) | copy-start | bytes 331780
  23.6 13.4 %all-to-all-start = ((f32[32,8,128]{2,1,0:T(8,128)}), f32[32,8,128]{2,1,0:T(8,128)S(1)}, u32[]{:S(2)}, u32[]{:S(2)}) async-start(f32[32,8,128]{2,1,0:T(8,128)} %bitcast.3), calls=%async_computation | async-start | bytes 262144 | tf_op jit(solution)/shard_map/all_to_all | solution.py:213
  27.6 9.5 %collective-permute-start.2 = (bf16[96,512]{1,0:T(8,128)(2,1)S(1)}, bf16[96,512]{1,0:T(8,128)(2,1)S(1)}, u32[]{:S(2)}, u32[]{:S(2)}) collective-permute-start(bf16[96,512]{1,0:T(8,128)(2,1)S(1)} %get-tuple-element.29.head_ref), channel_id=1, source_target_pairs={{1,0},{2,1},{3,2},{5,4},{6,5},{7,6},{9,8},{10,9},{11,10},{13,12},{... | collective-permute-start | bytes 294920 | tf_op jit(solution)/shard_map/ppermute | solution.py:232
  37.7 26.4 %all-to-all-start.1 = ((f32[16,8,128]{2,1,0:T(8,128)}), f32[16,8,128]{2,1,0:T(8,128)S(1)}, u32[]{:S(2)}, u32[]{:S(2)}) async-start(f32[16,8,128]{2,1,0:T(8,128)} %broadcast_in_dim.20), calls=%async_computation.1 | async-start | bytes 131072 | tf_op jit(solution)/shard_map/all_to_all | solution.py:213
  52.4 0.7 copy-start.2
  84.5 0.7 copy-start.1

commit v6 on v5

--- a/solution.py
+++ b/solution.py
@@ -234,7 +234,7 @@
     ahead = kernel.reshape(27 * cin, cout).T
     back = kernel[::-1].reshape(3, 9, cin, cout).transpose(1, 2, 0, 3).reshape(9 * cin, 3 * cout)
     bias = channel_bias[:, None]
-    part, hi, ahead, back, bias = lax.optimization_barrier((jnp.sum(parts, axis=0), hi, ahead, back, bias))
+    part, ahead, back, bias = lax.optimization_barrier((jnp.sum(parts, axis=0), ahead, back, bias))
     planes = (lo, head, mid, tail, hi)
     output = forward(cin, planes, ahead, bias, part)
     grad_input = backward(cin, planes, back, part)
@@ -245,7 +245,7 @@
     last = core * TILES + lax.axis_index(NEAR) >= BIAS_ROW // 8 * (cin // 2)
     rest = last & (lax.broadcasted_iota(jnp.int32, part.shape, 0) == (BIAS_ROW + 1) % 8)
     part = jnp.where(rest, part - rounded, rounded).astype(jnp.bfloat16)
-    total = lax.all_gather(swap(jnp.broadcast_to(part, tiles.shape), NEAR), CORE).astype(jnp.float32)
+    total = swap(jnp.broadcast_to(part, (2 * TILES, *part.shape)), (CORE, *NEAR)).astype(jnp.float32)
     total = total.reshape(4, 16, 8, 128).transpose(0, 2, 1, 3).reshape(ROWS, 2048)
     bias_total = total[BIAS_ROW, :cout] + total[BIAS_ROW + 1, :cout]
     return (output[None], grad_input[None], total[:27], bias_total)

time: 85.6 us -> 82.9 us (0.968)
  blocking collectives: 20.2 us -> 17.6 us
    all_gather x1 -> x0, blocking collectives: 6.34 us -> none  [on_device(): lax.all_gather(swap(jnp.broadcast_to(part, tiles.shape), NEAR), CORE)]
    ppermute x1, waiting for transfers between devices: 0.01 us -> 3.94 us  [on_device(): hi = lax.ppermute(head_late, 'gz', [(i + 1, i) for i in range(slabs - 1)])]
    all_to_all x1, blocking collectives: 13.9 us -> 17.6 us  [swap(): return lax.all_to_all(blocks, axes, 0, 0, tiled=True)]
    all_to_all x2, waiting for transfers between devices: 14.8 us -> 11.5 us  [swap(): return lax.all_to_all(blocks, axes, 0, 0, tiled=True)]
  transfers between devices with their start and end apart: 5 -> 5, of which waited for: 4 -> 5; matrix products, arithmetic and copies ran while one was open for 1% -> 1% of each run, Pallas kernels for 5% -> 5%
where the time goes in v6:
time: 82.9 us; the launch traced here: 82.6 us
  starting transfers between devices  37.9 us (46%)
  blocking collectives  17.6 us (21%)
  waiting for transfers between devices  16.9 us (20%)
  Pallas kernels  6.16 us (7%)
  local copies, waits for them, and re-layouts  1.83 us (2%)
  other arithmetic  1.38 us (2%)
    all_to_all x2, starting transfers between devices, swap(): return lax.all_to_all(blocks, axes, 0, 0, tiled=True)  18.7 us
    all_to_all x1, blocking collectives, swap(): return lax.all_to_all(blocks, axes, 0, 0, tiled=True)  17.6 us
    ppermute x1, starting transfers between devices, on_device(): lax.ppermute(send, CORE, [(0, 1), (1, 0)])  14 us
    all_to_all x2, waiting for transfers between devices, swap(): return lax.all_to_all(blocks, axes, 0, 0, tiled=True)  11.5 us
    pallas_call x5, Pallas kernels, call(): pl.pallas_call(body, out_shape=jax.tree.map(lambda s: pltpu.VMEM(s.shape,...  6.16 us
    ppermute x1, waiting for transfers between devices, on_device(): hi = lax.ppermute(head_late, 'gz', [(i + 1, i) for i in range(slabs - 1)])  3.94 us
    ppermute x1, starting transfers between devices, on_device(): lo = lax.ppermute(tail, 'gz', [(i, i + 1) for i in range(slabs - 1)])  3.94 us
  transfers between devices with their start and end apart: 5, of which 5 were waited for; matrix products, arithmetic and copies ran while one was open for 1% of the time, Pallas kernels for 5%

profile of v6, /device:TPU:1, one launch (start us, length us, event | category | flops | bytes accessed | tf_op | source)
XLA Modules:
  0.0 82.6 jit_solution(13555857525032219597)
XLA Ops:
  0.6 1.2 %shard_map.75 = (bf16[96,512]{1,0:T(8,128)(2,1)S(1)}, bf16[2,96,512]{2,1,0:T(8,128)(2,1)S(1)}, bf16[96,512]{1,0:T(8,128)(2,1)S(1)}) custom-call(bf16[32,4,512]{2,1,0:T(4,128)(2,1)} %bitcast.26, bf16[64,4,512]{2,1,0:T(4,128)(2,1)} %bitcast.23), custom_call_target="tpu_custom_call" | custom-call | tf_op jit(solution)/shard_map/pallas_call | solution.py:29
  1.8 3.9 %collective-permute-start = (bf16[96,512]{1,0:T(8,128)(2,1)S(1)}, bf16[96,512]{1,0:T(8,128)(2,1)S(1)}, u32[]{:S(2)}, u32[]{:S(2)}) collective-permute-start(bf16[96,512]{1,0:T(8,128)(2,1)S(1)} %get-tuple-element.20.tail_ref), channel_id=1, source_target_pairs={{0,1},{1,2},{2,3},{4,5},{5,6},{6,7},{8,9},{9,10},{10,11},{12,13},{... | collective-permute-start | bytes 294920 | tf_op jit(solution)/shard_map/below/ppermute | solution.py:225
  5.8 1.1 %shard_map.76 = (f32[1024,128]{1,0:T(8,128)S(1)}, bf16[288,512]{1,0:T(8,128)(2,1)S(1)}) custom-call(bf16[96,512]{1,0:T(8,128)(2,1)S(1)} %get-tuple-element.29.head_ref, bf16[2,96,512]{2,1,0:T(8,128)(2,1)S(1)} %get-tuple-element.22.mid_ref, bf16[96,512]{1,0:T(8,128)(2,1)S(1)} %get-tuple-element.20.tail_ref), custom_call_target="tpu_custom_call" | custom-call | tf_op jit(solution)/shard_map/pallas_call | solution.py:29
  6.9 0.5 collective-permute-done.lo_ref
  7.4 0.6 shard_map.77
  8.0 14.0 %collective-permute-start.1 = (f32[2,16,8,128]{3,2,1,0:T(8,128)S(1)}, f32[2,16,8,128]{3,2,1,0:T(8,128)S(1)}, u32[]{:S(2)}, u32[]{:S(2)}) collective-permute-start(f32[2,16,8,128]{3,2,1,0:T(8,128)S(1)} %get-tuple-element.26), channel_id=1, source_target_pairs={{0,4},{4,0},{1,5},{5,1},{2,6},{6,2},{3,7},{7,3},{8,12},{12,8},{9,1... | collective-permute-start | bytes 393224 | tf_op jit(solution)/shard_map/ppermute | solution.py:229
  22.0 1.0 %collective-permute-done.1 = f32[2,16,8,128]{3,2,1,0:T(8,128)S(1)} collective-permute-done((f32[2,16,8,128]{3,2,1,0:T(8,128)S(1)}, f32[2,16,8,128]{3,2,1,0:T(8,128)S(1)}, u32[]{:S(2)}, u32[]{:S(2)}) %collective-permute-start.1) | collective-permute-done | bytes 131104 | tf_op jit(solution)/shard_map/ppermute | solution.py:229
  22.9 0.7 add.15
  23.6 0.0 copy-start
  23.6 4.0 %all-to-all-start = ((f32[32,8,128]{2,1,0:T(8,128)}), f32[32,8,128]{2,1,0:T(8,128)S(1)}, u32[]{:S(2)}, u32[]{:S(2)}) async-start(f32[32,8,128]{2,1,0:T(8,128)} %bitcast.3), calls=%async_computation | async-start | bytes 262144 | tf_op jit(solution)/shard_map/all_to_all | solution.py:213
  27.6 0.0 copy-done
  27.6 0.2 reshape.32
  27.8 0.2 reshape_reshape.3
  28.1 0.2 copy.13
  28.2 0.2 reshape.34.w_ref
  28.4 0.1 copy.12
  28.6 8.5 %all-to-all-done = f32[32,8,128]{2,1,0:T(8,128)S(1)} async-done(((f32[32,8,128]{2,1,0:T(8,128)}), f32[32,8,128]{2,1,0:T(8,128)S(1)}, u32[]{:S(2)}, u32[]{:S(2)}) %all-to-all-start) | async-done | bytes 131104 | tf_op jit(solution)/shard_map/all_to_all | solution.py:213
  37.1 0.6 broadcast_in_dim.20
  37.7 14.7 %all-to-all-start.1 = ((f32[16,8,128]{2,1,0:T(8,128)}), f32[16,8,128]{2,1,0:T(8,128)S(1)}, u32[]{:S(2)}, u32[]{:S(2)}) async-start(f32[16,8,128]{2,1,0:T(8,128)} %broadcast_in_dim.20), calls=%async_computation.1 | async-start | bytes 131072 | tf_op jit(solution)/shard_map/all_to_all | solution.py:213
  52.4 0.0 copy-start.2
  52.5 1.3 %collective-permute-start.2 = (bf16[96,512]{1,0:T(8,128)(2,1)S(1)}, bf16[96,512]{1,0:T(8,128)(2,1)S(1)}, u32[]{:S(2)}, u32[]{:S(2)}) collective-permute-start(bf16[96,512]{1,0:T(8,128)(2,1)S(1)} %get-tuple-element.29.head_ref), channel_id=1, source_target_pairs={{1,0},{2,1},{3,2},{5,4},{6,5},{7,6},{9,8},{10,9},{11,10},{13,12},{... | collective-permute-start | bytes 294920 | tf_op jit(solution)/shard_map/ppermute | solution.py:232
  53.8 0.0 copy-done.2
  53.8 0.1 copy.14.bias_ref
  53.9 3.9 %collective-permute-done.2.hi_ref = bf16[96,512]{1,0:T(8,128)(2,1)S(1)} collective-permute-done((bf16[96,512]{1,0:T(8,128)(2,1)S(1)}, bf16[96,512]{1,0:T(8,128)(2,1)S(1)}, u32[]{:S(2)}, u32[]{:S(2)}) %collective-permute-start.2) | collective-permute-done | bytes 98336 | tf_op jit(solution)/shard_map/ppermute | solution.py:232
  57.8 1.6 %shard_map.79 = bf16[32,4,512]{2,1,0:T(4,128)(2,1)} custom-call(bf16[96,512]{1,0:T(8,128)(2,1)S(1)} %collective-permute-done.lo_ref, bf16[96,512]{1,0:T(8,128)(2,1)S(1)} %get-tuple-element.29.head_ref, bf16[2,96,512]{2,1,0:T(8,128)(2,1)S(1)} %get-tuple-element.22.mid_ref, bf16[96,512]{1,0:T(8,128)(2,1)S(1)} %get-tuple-element.20.tail_ref, ...), custom_call_target="tpu_custom_call" | custom-call | tf_op jit(solution)/shard_map/pallas_call | solution.py:29
  59.4 1.7 %shard_map.78 = bf16[64,4,512]{2,1,0:T(4,128)(2,1)} custom-call(bf16[96,512]{1,0:T(8,128)(2,1)S(1)} %collective-permute-done.lo_ref, bf16[96,512]{1,0:T(8,128)(2,1)S(1)} %get-tuple-element.29.head_ref, bf16[2,96,512]{2,1,0:T(8,128)(2,1)S(1)} %get-tuple-element.22.mid_ref, bf16[96,512]{1,0:T(8,128)(2,1)S(1)} %get-tuple-element.20.tail_ref, ...), custom_call_target="tpu_custom_call" | custom-call | tf_op jit(solution)/shard_map/pallas_call | solution.py:29
  61.1 3.0 %all-to-all-done.1 = f32[16,8,128]{2,1,0:T(8,128)S(1)} async-done(((f32[16,8,128]{2,1,0:T(8,128)}), f32[16,8,128]{2,1,0:T(8,128)S(1)}, u32[]{:S(2)}, u32[]{:S(2)}) %all-to-all-start.1) | async-done | bytes 65568 | tf_op jit(solution)/shard_map/all_to_all | solution.py:213
  64.1 0.1 fusion
  64.2 17.6 %all_to_all.15 = bf16[64,8,128]{2,1,0:T(8,128)(2,1)S(1)} all-to-all(bf16[64,8,128]{2,1,0:T(8,128)(2,1)S(1)} %broadcast_in_dim.23), channel_id=1, replica_groups=mesh['dp_0'=16,'dp_1'=8,'dp_2'=2,'gz'=4] {'dp_2','dp_1','gz'}, dimensions={0} | all-to-all | bytes 262144 | tf_op jit(solution)/shard_map/all_to_all | solution.py:213
  81.9 0.0 copy-start.1
  81.9 0.6 fusion.1
  82.4 0.1 copy-done.1
  (6 shorter events, 0.1 us)
Async XLA Ops:
  1.8 5.6 %collective-permute-start = (bf16[96,512]{1,0:T(8,128)(2,1)S(1)}, bf16[96,512]{1,0:T(8,128)(2,1)S(1)}, u32[]{:S(2)}, u32[]{:S(2)}) collective-permute-start(bf16[96,512]{1,0:T(8,128)(2,1)S(1)} %get-tuple-element.20.tail_ref), channel_id=1, source_target_pairs={{0,1},{1,2},{2,3},{4,5},{5,6},{6,7},{8,9},{9,10},{10,11},{12,13},{... | collective-permute-start | bytes 294920 | tf_op jit(solution)/shard_map/below/ppermute | solution.py:225
  8.0 14.9 %collective-permute-start.1 = (f32[2,16,8,128]{3,2,1,0:T(8,128)S(1)}, f32[2,16,8,128]{3,2,1,0:T(8,128)S(1)}, u32[]{:S(2)}, u32[]{:S(2)}) collective-permute-start(f32[2,16,8,128]{3,2,1,0:T(8,128)S(1)} %get-tuple-element.26), channel_id=1, source_target_pairs={{0,4},{4,0},{1,5},{5,1},{2,6},{6,2},{3,7},{7,3},{8,12},{12,8},{9,1... | collective-permute-start | bytes 393224 | tf_op jit(solution)/shard_map/ppermute | solution.py:229
  23.6 4.0 %copy-start = (bf16[27,2048]{1,0:T(8,128)(2,1)S(1)}, bf16[27,2048]{1,0:T(8,128)(2,1)}, u32[]{:S(2)}) copy-start(bf16[27,2048]{1,0:T(8,128)(2,1)} %param.5) | copy-start | bytes 331780
  23.6 13.4 %all-to-all-start = ((f32[32,8,128]{2,1,0:T(8,128)}), f32[32,8,128]{2,1,0:T(8,128)S(1)}, u32[]{:S(2)}, u32[]{:S(2)}) async-start(f32[32,8,128]{2,1,0:T(8,128)} %bitcast.3), calls=%async_computation | async-start | bytes 262144 | tf_op jit(solution)/shard_map/all_to_all | solution.py:213
  37.7 26.4 %all-to-all-start.1 = ((f32[16,8,128]{2,1,0:T(8,128)}), f32[16,8,128]{2,1,0:T(8,128)S(1)}, u32[]{:S(2)}, u32[]{:S(2)}) async-start(f32[16,8,128]{2,1,0:T(8,128)} %broadcast_in_dim.20), calls=%async_computation.1 | async-start | bytes 131072 | tf_op jit(solution)/shard_map/all_to_all | solution.py:213
  52.4 1.3 %copy-start.2 = (f32[64]{0:T(128)S(1)}, f32[64]{0:T(128)}, u32[]{:S(2)}) copy-start(f32[64]{0:T(128)} %param.6) | copy-start | bytes 772
  52.5 5.4 %collective-permute-start.2 = (bf16[96,512]{1,0:T(8,128)(2,1)S(1)}, bf16[96,512]{1,0:T(8,128)(2,1)S(1)}, u32[]{:S(2)}, u32[]{:S(2)}) collective-permute-start(bf16[96,512]{1,0:T(8,128)(2,1)S(1)} %get-tuple-element.29.head_ref), channel_id=1, source_target_pairs={{1,0},{2,1},{3,2},{5,4},{6,5},{7,6},{9,8},{10,9},{11,10},{13,12},{... | collective-permute-start | bytes 294920 | tf_op jit(solution)/shard_map/ppermute | solution.py:232
  81.9 0.7 copy-start.1

commit v7 on v6

--- a/solution.py
+++ b/solution.py
@@ -8,6 +8,7 @@
 from jax.experimental.pallas import tpu as pltpu
 from jax.sharding import Mesh
 from jax.sharding import PartitionSpec as P
+
 
 NX = 64
 NY = 8
@@ -221,8 +222,7 @@
     factor = 1.0 / math.sqrt(cells_all)
     head, mid, tail = split_planes(feats, grads)
     slabs = lax.axis_size("gz")
-    with jax.named_scope("below"):
-        lo = lax.ppermute(tail, "gz", [(i, i + 1) for i in range(slabs - 1)])
+    lo = lax.ppermute(tail, "gz", [(i, i + 1) for i in range(slabs - 1)])
     own, head_moved = own_terms(cin, head, mid, tail)
     core = lax.axis_index(CORE)
     keep, send = weight_tiles(cin, core[None], lo, head, head_moved, own, factor)
@@ -239,7 +239,9 @@
     output = forward(cin, planes, ahead, bias, part)
     grad_input = backward(cin, planes, back, part)
     far = lax.axis_size("dp_0")
-    part = jnp.sum(swap(jnp.broadcast_to(part, (far, *part.shape)), "dp_0"), axis=0)
+    part = jnp.broadcast_to(part, (far, *part.shape))
+    part = swap(part, "dp_0")
+    part = jnp.sum(part, axis=0)
     part, output, grad_input = lax.optimization_barrier((part, output, grad_input))
     rounded = lax.reduce_precision(part, 8, 7)
     last = core * TILES + lax.axis_index(NEAR) >= BIAS_ROW // 8 * (cin // 2)

time: 82.9 us -> 82.9 us (level)
  no operation moved by 1% of the time
where the time goes in v7:
time: 82.9 us; the launch traced here: 82.6 us
  starting transfers between devices  37.9 us (46%)
  blocking collectives  17.6 us (21%)
  waiting for transfers between devices  16.9 us (20%)
  Pallas kernels  6.16 us (7%)
  local copies, waits for them, and re-layouts  1.83 us (2%)
  other arithmetic  1.38 us (2%)
    all_to_all x2, starting transfers between devices, swap(): return lax.all_to_all(blocks, axes, 0, 0, tiled=True)  18.7 us
    all_to_all x1, blocking collectives, swap(): return lax.all_to_all(blocks, axes, 0, 0, tiled=True)  17.6 us
    ppermute x1, starting transfers between devices, on_device(): lax.ppermute(send, CORE, [(0, 1), (1, 0)])  14 us
    all_to_all x2, waiting for transfers between devices, swap(): return lax.all_to_all(blocks, axes, 0, 0, tiled=True)  11.5 us
    pallas_call x5, Pallas kernels, call(): pl.pallas_call(body, out_shape=jax.tree.map(lambda s: pltpu.VMEM(s.shape,...  6.16 us
    ppermute x1, waiting for transfers between devices, on_device(): hi = lax.ppermute(head_late, 'gz', [(i + 1, i) for i in range(slabs - 1)])  3.94 us
    ppermute x1, starting transfers between devices, on_device(): lo = lax.ppermute(tail, 'gz', [(i, i + 1) for i in range(slabs - 1)])  3.94 us
  transfers between devices with their start and end apart: 5, of which 5 were waited for; matrix products, arithmetic and copies ran while one was open for 1% of the time, Pallas kernels for 5%

profile of v7, /device:TPU:1, one launch (start us, length us, event | category | flops | bytes accessed | tf_op | source)
XLA Modules:
  0.0 82.6 jit_solution(13555857525032219597)
XLA Ops:
  0.6 1.2 %shard_map.75 = (bf16[96,512]{1,0:T(8,128)(2,1)S(1)}, bf16[2,96,512]{2,1,0:T(8,128)(2,1)S(1)}, bf16[96,512]{1,0:T(8,128)(2,1)S(1)}) custom-call(bf16[32,4,512]{2,1,0:T(4,128)(2,1)} %bitcast.26, bf16[64,4,512]{2,1,0:T(4,128)(2,1)} %bitcast.23), custom_call_target="tpu_custom_call" | custom-call | tf_op jit(solution)/shard_map/pallas_call | solution.py:30
  1.8 3.9 %collective-permute-start = (bf16[96,512]{1,0:T(8,128)(2,1)S(1)}, bf16[96,512]{1,0:T(8,128)(2,1)S(1)}, u32[]{:S(2)}, u32[]{:S(2)}) collective-permute-start(bf16[96,512]{1,0:T(8,128)(2,1)S(1)} %get-tuple-element.20.tail_ref), channel_id=1, source_target_pairs={{0,1},{1,2},{2,3},{4,5},{5,6},{6,7},{8,9},{9,10},{10,11},{12,13},{... | collective-permute-start | bytes 294920 | tf_op jit(solution)/shard_map/ppermute | solution.py:225
  5.8 1.1 %shard_map.76 = (f32[1024,128]{1,0:T(8,128)S(1)}, bf16[288,512]{1,0:T(8,128)(2,1)S(1)}) custom-call(bf16[96,512]{1,0:T(8,128)(2,1)S(1)} %get-tuple-element.29.head_ref, bf16[2,96,512]{2,1,0:T(8,128)(2,1)S(1)} %get-tuple-element.22.mid_ref, bf16[96,512]{1,0:T(8,128)(2,1)S(1)} %get-tuple-element.20.tail_ref), custom_call_target="tpu_custom_call" | custom-call | tf_op jit(solution)/shard_map/pallas_call | solution.py:30
  6.9 0.5 collective-permute-done.lo_ref
  7.4 0.6 shard_map.77
  8.0 14.0 %collective-permute-start.1 = (f32[2,16,8,128]{3,2,1,0:T(8,128)S(1)}, f32[2,16,8,128]{3,2,1,0:T(8,128)S(1)}, u32[]{:S(2)}, u32[]{:S(2)}) collective-permute-start(f32[2,16,8,128]{3,2,1,0:T(8,128)S(1)} %get-tuple-element.26), channel_id=1, source_target_pairs={{0,4},{4,0},{1,5},{5,1},{2,6},{6,2},{3,7},{7,3},{8,12},{12,8},{9,1... | collective-permute-start | bytes 393224 | tf_op jit(solution)/shard_map/ppermute | solution.py:229
  22.0 1.0 %collective-permute-done.1 = f32[2,16,8,128]{3,2,1,0:T(8,128)S(1)} collective-permute-done((f32[2,16,8,128]{3,2,1,0:T(8,128)S(1)}, f32[2,16,8,128]{3,2,1,0:T(8,128)S(1)}, u32[]{:S(2)}, u32[]{:S(2)}) %collective-permute-start.1) | collective-permute-done | bytes 131104 | tf_op jit(solution)/shard_map/ppermute | solution.py:229
  22.9 0.7 add.15
  23.6 0.0 copy-start
  23.6 4.0 %all-to-all-start = ((f32[32,8,128]{2,1,0:T(8,128)}), f32[32,8,128]{2,1,0:T(8,128)S(1)}, u32[]{:S(2)}, u32[]{:S(2)}) async-start(f32[32,8,128]{2,1,0:T(8,128)} %bitcast.3), calls=%async_computation | async-start | bytes 262144 | tf_op jit(solution)/shard_map/all_to_all | solution.py:214
  27.6 0.0 copy-done
  27.6 0.2 reshape.32
  27.8 0.2 reshape_reshape.3
  28.1 0.2 copy.13
  28.2 0.2 reshape.34.w_ref
  28.4 0.1 copy.12
  28.6 8.5 %all-to-all-done = f32[32,8,128]{2,1,0:T(8,128)S(1)} async-done(((f32[32,8,128]{2,1,0:T(8,128)}), f32[32,8,128]{2,1,0:T(8,128)S(1)}, u32[]{:S(2)}, u32[]{:S(2)}) %all-to-all-start) | async-done | bytes 131104 | tf_op jit(solution)/shard_map/all_to_all | solution.py:214
  37.1 0.6 broadcast_in_dim.20
  37.7 14.7 %all-to-all-start.1 = ((f32[16,8,128]{2,1,0:T(8,128)}), f32[16,8,128]{2,1,0:T(8,128)S(1)}, u32[]{:S(2)}, u32[]{:S(2)}) async-start(f32[16,8,128]{2,1,0:T(8,128)} %broadcast_in_dim.20), calls=%async_computation.1 | async-start | bytes 131072 | tf_op jit(solution)/shard_map/all_to_all | solution.py:214
  52.4 0.0 copy-start.2
  52.5 1.3 %collective-permute-start.2 = (bf16[96,512]{1,0:T(8,128)(2,1)S(1)}, bf16[96,512]{1,0:T(8,128)(2,1)S(1)}, u32[]{:S(2)}, u32[]{:S(2)}) collective-permute-start(bf16[96,512]{1,0:T(8,128)(2,1)S(1)} %get-tuple-element.29.head_ref), channel_id=1, source_target_pairs={{1,0},{2,1},{3,2},{5,4},{6,5},{7,6},{9,8},{10,9},{11,10},{13,12},{... | collective-permute-start | bytes 294920 | tf_op jit(solution)/shard_map/ppermute | solution.py:232
  53.8 0.0 copy-done.2
  53.8 0.1 copy.14.bias_ref
  53.9 3.9 %collective-permute-done.2.hi_ref = bf16[96,512]{1,0:T(8,128)(2,1)S(1)} collective-permute-done((bf16[96,512]{1,0:T(8,128)(2,1)S(1)}, bf16[96,512]{1,0:T(8,128)(2,1)S(1)}, u32[]{:S(2)}, u32[]{:S(2)}) %collective-permute-start.2) | collective-permute-done | bytes 98336 | tf_op jit(solution)/shard_map/ppermute | solution.py:232
  57.8 1.6 %shard_map.79 = bf16[32,4,512]{2,1,0:T(4,128)(2,1)} custom-call(bf16[96,512]{1,0:T(8,128)(2,1)S(1)} %collective-permute-done.lo_ref, bf16[96,512]{1,0:T(8,128)(2,1)S(1)} %get-tuple-element.29.head_ref, bf16[2,96,512]{2,1,0:T(8,128)(2,1)S(1)} %get-tuple-element.22.mid_ref, bf16[96,512]{1,0:T(8,128)(2,1)S(1)} %get-tuple-element.20.tail_ref, ...), custom_call_target="tpu_custom_call" | custom-call | tf_op jit(solution)/shard_map/pallas_call | solution.py:30
  59.4 1.7 %shard_map.78 = bf16[64,4,512]{2,1,0:T(4,128)(2,1)} custom-call(bf16[96,512]{1,0:T(8,128)(2,1)S(1)} %collective-permute-done.lo_ref, bf16[96,512]{1,0:T(8,128)(2,1)S(1)} %get-tuple-element.29.head_ref, bf16[2,96,512]{2,1,0:T(8,128)(2,1)S(1)} %get-tuple-element.22.mid_ref, bf16[96,512]{1,0:T(8,128)(2,1)S(1)} %get-tuple-element.20.tail_ref, ...), custom_call_target="tpu_custom_call" | custom-call | tf_op jit(solution)/shard_map/pallas_call | solution.py:30
  61.1 3.0 %all-to-all-done.1 = f32[16,8,128]{2,1,0:T(8,128)S(1)} async-done(((f32[16,8,128]{2,1,0:T(8,128)}), f32[16,8,128]{2,1,0:T(8,128)S(1)}, u32[]{:S(2)}, u32[]{:S(2)}) %all-to-all-start.1) | async-done | bytes 65568 | tf_op jit(solution)/shard_map/all_to_all | solution.py:214
  64.1 0.1 fusion
  64.2 17.6 %all_to_all.15 = bf16[64,8,128]{2,1,0:T(8,128)(2,1)S(1)} all-to-all(bf16[64,8,128]{2,1,0:T(8,128)(2,1)S(1)} %broadcast_in_dim.23), channel_id=1, replica_groups=mesh['dp_0'=16,'dp_1'=8,'dp_2'=2,'gz'=4] {'dp_2','dp_1','gz'}, dimensions={0} | all-to-all | bytes 262144 | tf_op jit(solution)/shard_map/all_to_all | solution.py:214
  81.9 0.0 copy-start.1
  81.9 0.6 fusion.1
  82.4 0.1 copy-done.1
  (6 shorter events, 0.1 us)
Async XLA Ops:
  1.8 5.6 %collective-permute-start = (bf16[96,512]{1,0:T(8,128)(2,1)S(1)}, bf16[96,512]{1,0:T(8,128)(2,1)S(1)}, u32[]{:S(2)}, u32[]{:S(2)}) collective-permute-start(bf16[96,512]{1,0:T(8,128)(2,1)S(1)} %get-tuple-element.20.tail_ref), channel_id=1, source_target_pairs={{0,1},{1,2},{2,3},{4,5},{5,6},{6,7},{8,9},{9,10},{10,11},{12,13},{... | collective-permute-start | bytes 294920 | tf_op jit(solution)/shard_map/ppermute | solution.py:225
  8.0 14.9 %collective-permute-start.1 = (f32[2,16,8,128]{3,2,1,0:T(8,128)S(1)}, f32[2,16,8,128]{3,2,1,0:T(8,128)S(1)}, u32[]{:S(2)}, u32[]{:S(2)}) collective-permute-start(f32[2,16,8,128]{3,2,1,0:T(8,128)S(1)} %get-tuple-element.26), channel_id=1, source_target_pairs={{0,4},{4,0},{1,5},{5,1},{2,6},{6,2},{3,7},{7,3},{8,12},{12,8},{9,1... | collective-permute-start | bytes 393224 | tf_op jit(solution)/shard_map/ppermute | solution.py:229
  23.6 4.0 %copy-start = (bf16[27,2048]{1,0:T(8,128)(2,1)S(1)}, bf16[27,2048]{1,0:T(8,128)(2,1)}, u32[]{:S(2)}) copy-start(bf16[27,2048]{1,0:T(8,128)(2,1)} %param.5) | copy-start | bytes 331780
  23.6 13.4 %all-to-all-start = ((f32[32,8,128]{2,1,0:T(8,128)}), f32[32,8,128]{2,1,0:T(8,128)S(1)}, u32[]{:S(2)}, u32[]{:S(2)}) async-start(f32[32,8,128]{2,1,0:T(8,128)} %bitcast.3), calls=%async_computation | async-start | bytes 262144 | tf_op jit(solution)/shard_map/all_to_all | solution.py:214
  37.7 26.4 %all-to-all-start.1 = ((f32[16,8,128]{2,1,0:T(8,128)}), f32[16,8,128]{2,1,0:T(8,128)S(1)}, u32[]{:S(2)}, u32[]{:S(2)}) async-start(f32[16,8,128]{2,1,0:T(8,128)} %broadcast_in_dim.20), calls=%async_computation.1 | async-start | bytes 131072 | tf_op jit(solution)/shard_map/all_to_all | solution.py:214
  52.4 1.3 %copy-start.2 = (f32[64]{0:T(128)S(1)}, f32[64]{0:T(128)}, u32[]{:S(2)}) copy-start(f32[64]{0:T(128)} %param.6) | copy-start | bytes 772
  52.5 5.4 %collective-permute-start.2 = (bf16[96,512]{1,0:T(8,128)(2,1)S(1)}, bf16[96,512]{1,0:T(8,128)(2,1)S(1)}, u32[]{:S(2)}, u32[]{:S(2)}) collective-permute-start(bf16[96,512]{1,0:T(8,128)(2,1)S(1)} %get-tuple-element.29.head_ref), channel_id=1, source_target_pairs={{1,0},{2,1},{3,2},{5,4},{6,5},{7,6},{9,8},{10,9},{11,10},{13,12},{... | collective-permute-start | bytes 294920 | tf_op jit(solution)/shard_map/ppermute | solution.py:232
  81.9 0.7 copy-start.1

commit v8 on v7

--- a/solution.py
+++ b/solution.py
@@ -223,18 +223,18 @@
     head, mid, tail = split_planes(feats, grads)
     slabs = lax.axis_size("gz")
     lo = lax.ppermute(tail, "gz", [(i, i + 1) for i in range(slabs - 1)])
+    hi = lax.ppermute(head, "gz", [(i + 1, i) for i in range(slabs - 1)])
     own, head_moved = own_terms(cin, head, mid, tail)
     core = lax.axis_index(CORE)
     keep, send = weight_tiles(cin, core[None], lo, head, head_moved, own, factor)
-    tiles = (keep + lax.ppermute(send, CORE, [(0, 1), (1, 0)])).reshape(TILES, 8, 128)
-    tiles, head_late = lax.optimization_barrier((tiles, head))
+    other = lax.ppermute(send, CORE, [(0, 1), (1, 0)])
+    tiles = (keep + other).reshape(TILES, 8, 128)
     parts = swap(tiles, NEAR)
-    hi = lax.ppermute(head_late, "gz", [(i + 1, i) for i in range(slabs - 1)])
+    part, kernel_taps, channel_bias = lax.optimization_barrier((jnp.sum(parts, axis=0), kernel_taps, channel_bias))
     kernel = kernel_taps.reshape(27, cin, cout)
     ahead = kernel.reshape(27 * cin, cout).T
     back = kernel[::-1].reshape(3, 9, cin, cout).transpose(1, 2, 0, 3).reshape(9 * cin, 3 * cout)
     bias = channel_bias[:, None]
-    part, ahead, back, bias = lax.optimization_barrier((jnp.sum(parts, axis=0), ahead, back, bias))
     planes = (lo, head, mid, tail, hi)
     output = forward(cin, planes, ahead, bias, part)
     grad_input = backward(cin, planes, back, part)

time: 82.9 us -> 81.9 us (0.988)
  blocking collectives: 17.6 us -> 30.6 us
  waiting for transfers between devices: 16.9 us -> 6.83 us
  starting transfers between devices: 37.9 us -> 34 us
    all_to_all x1 -> x2, blocking collectives: 17.6 us -> 30.6 us  [swap(): return lax.all_to_all(blocks, axes, 0, 0, tiled=True)]
    all_to_all x2 -> x1, waiting for transfers between devices: 11.5 us -> 3.03 us  [swap(): return lax.all_to_all(blocks, axes, 0, 0, tiled=True)]
    all_to_all x2 -> x1, starting transfers between devices: 18.7 us -> 14.9 us  [swap(): return lax.all_to_all(blocks, axes, 0, 0, tiled=True)]
    ppermute x2, waiting for transfers between devices: 4.91 us -> 3.28 us  [the longest x1 2.32 us: on_device(): hi = lax.ppermute(head, 'gz', [(i + 1, i) for i in range(slabs - 1)])]
  transfers between devices with their start and end apart: 5 -> 4, of which waited for: 5 -> 4; matrix products, arithmetic and copies ran while one was open for 1% -> 1% of each run, Pallas kernels for 5% -> 5%
where the time goes in v8:
time: 81.9 us; the launch traced here: 81.6 us
  starting transfers between devices  34 us (42%)
  blocking collectives  30.6 us (37%)
  waiting for transfers between devices  6.83 us (8%)
  Pallas kernels  6.17 us (8%)
  local copies, waits for them, and re-layouts  2.47 us (3%)
    all_to_all x2, blocking collectives, swap(): return lax.all_to_all(blocks, axes, 0, 0, tiled=True)  30.6 us
    all_to_all x1, starting transfers between devices, swap(): return lax.all_to_all(blocks, axes, 0, 0, tiled=True)  14.9 us
    ppermute x1, starting transfers between devices, on_device(): other = lax.ppermute(send, CORE, [(0, 1), (1, 0)])  14 us
    pallas_call x5, Pallas kernels, call(): pl.pallas_call(body, out_shape=jax.tree.map(lambda s: pltpu.VMEM(s.shape,...  6.17 us
    ppermute x1, starting transfers between devices, on_device(): lo = lax.ppermute(tail, 'gz', [(i, i + 1) for i in range(slabs - 1)])  3.94 us
    all_to_all x1, waiting for transfers between devices, swap(): return lax.all_to_all(blocks, axes, 0, 0, tiled=True)  3.03 us
    ppermute x1, waiting for transfers between devices, on_device(): hi = lax.ppermute(head, 'gz', [(i + 1, i) for i in range(slabs - 1)])  2.32 us
  transfers between devices with their start and end apart: 4, of which 4 were waited for; matrix products, arithmetic and copies ran while one was open for 1% of the time, Pallas kernels for 5%

profile of v8, /device:TPU:1, one launch (start us, length us, event | category | flops | bytes accessed | tf_op | source)
XLA Modules:
  0.0 81.6 jit_solution(17455524362271428722)
XLA Ops:
  0.6 1.2 %shard_map.75 = (bf16[96,512]{1,0:T(8,128)(2,1)S(1)}, bf16[2,96,512]{2,1,0:T(8,128)(2,1)S(1)}, bf16[96,512]{1,0:T(8,128)(2,1)S(1)}) custom-call(bf16[32,4,512]{2,1,0:T(4,128)(2,1)} %bitcast.27, bf16[64,4,512]{2,1,0:T(4,128)(2,1)} %bitcast.24), custom_call_target="tpu_custom_call" | custom-call | tf_op jit(solution)/shard_map/pallas_call | solution.py:30
  1.8 3.9 %collective-permute-start = (bf16[96,512]{1,0:T(8,128)(2,1)S(1)}, bf16[96,512]{1,0:T(8,128)(2,1)S(1)}, u32[]{:S(2)}, u32[]{:S(2)}) collective-permute-start(bf16[96,512]{1,0:T(8,128)(2,1)S(1)} %get-tuple-element.17.tail_ref), channel_id=1, source_target_pairs={{0,1},{1,2},{2,3},{4,5},{5,6},{6,7},{8,9},{9,10},{10,11},{12,13},{... | collective-permute-start | bytes 294920 | tf_op jit(solution)/shard_map/ppermute | solution.py:225
  5.8 1.1 %shard_map.76 = (f32[1024,128]{1,0:T(8,128)S(1)}, bf16[288,512]{1,0:T(8,128)(2,1)S(1)}) custom-call(bf16[96,512]{1,0:T(8,128)(2,1)S(1)} %get-tuple-element.18.head_ref, bf16[2,96,512]{2,1,0:T(8,128)(2,1)S(1)} %get-tuple-element.19.mid_ref, bf16[96,512]{1,0:T(8,128)(2,1)S(1)} %get-tuple-element.17.tail_ref), custom_call_target="tpu_custom_call" | custom-call | tf_op jit(solution)/shard_map/pallas_call | solution.py:30
  6.9 0.5 collective-permute-done.lo_ref
  7.4 0.6 shard_map.77
  8.0 14.0 %collective-permute-start.1 = (f32[2,16,8,128]{3,2,1,0:T(8,128)S(1)}, f32[2,16,8,128]{3,2,1,0:T(8,128)S(1)}, u32[]{:S(2)}, u32[]{:S(2)}) collective-permute-start(f32[2,16,8,128]{3,2,1,0:T(8,128)S(1)} %get-tuple-element.23), channel_id=1, source_target_pairs={{0,4},{4,0},{1,5},{5,1},{2,6},{6,2},{3,7},{7,3},{8,12},{12,8},{9,1... | collective-permute-start | bytes 393224 | tf_op jit(solution)/shard_map/ppermute | solution.py:230
  22.0 1.0 %collective-permute-done.1 = f32[2,16,8,128]{3,2,1,0:T(8,128)S(1)} collective-permute-done((f32[2,16,8,128]{3,2,1,0:T(8,128)S(1)}, f32[2,16,8,128]{3,2,1,0:T(8,128)S(1)}, u32[]{:S(2)}, u32[]{:S(2)}) %collective-permute-start.1) | collective-permute-done | bytes 131104 | tf_op jit(solution)/shard_map/ppermute | solution.py:230
  23.0 12.9 %all_to_all.15 = f32[32,8,128]{2,1,0:T(8,128)S(1)} all-to-all(f32[32,8,128]{2,1,0:T(8,128)S(1)} %bitcast.22), channel_id=1, replica_groups=mesh['dp_0'=16,'dp_1'=8,'dp_2'=2,'gz'=4] {'dp_1','gz'}, dimensions={0} | all-to-all | bytes 262144 | tf_op jit(solution)/shard_map/all_to_all | solution.py:214
  35.9 0.0 copy-start
  35.9 0.6 broadcast_in_dim.19
  36.6 14.9 %all-to-all-start.1 = ((f32[16,8,128]{2,1,0:T(8,128)}), f32[16,8,128]{2,1,0:T(8,128)S(1)}, u32[]{:S(2)}, u32[]{:S(2)}) async-start(f32[16,8,128]{2,1,0:T(8,128)} %broadcast_in_dim.19), calls=%async_computation.1 | async-start | bytes 131072 | tf_op jit(solution)/shard_map/all_to_all | solution.py:214
  51.4 1.3 %collective-permute-start.2 = (bf16[96,512]{1,0:T(8,128)(2,1)S(1)}, bf16[96,512]{1,0:T(8,128)(2,1)S(1)}, u32[]{:S(2)}, u32[]{:S(2)}) collective-permute-start(bf16[96,512]{1,0:T(8,128)(2,1)S(1)} %get-tuple-element.18.head_ref), channel_id=1, source_target_pairs={{1,0},{2,1},{3,2},{5,4},{6,5},{7,6},{9,8},{10,9},{11,10},{13,12},{... | collective-permute-start | bytes 294920 | tf_op jit(solution)/shard_map/ppermute | solution.py:226
  52.8 0.0 copy-done
  52.8 0.2 reshape.32
  53.0 0.2 reshape_reshape.3
  53.2 0.2 copy.14
  53.4 0.2 reshape.34.w_ref
  53.6 0.1 copy.12
  53.7 0.0 copy-start.2
  53.7 0.6 copy-done.2
  54.4 0.1 copy.13.bias_ref
  54.5 2.3 %collective-permute-done.2.hi_ref = bf16[96,512]{1,0:T(8,128)(2,1)S(1)} collective-permute-done((bf16[96,512]{1,0:T(8,128)(2,1)S(1)}, bf16[96,512]{1,0:T(8,128)(2,1)S(1)}, u32[]{:S(2)}, u32[]{:S(2)}) %collective-permute-start.2) | collective-permute-done | bytes 98336 | tf_op jit(solution)/shard_map/ppermute | solution.py:226
  56.8 1.6 %shard_map.79 = bf16[32,4,512]{2,1,0:T(4,128)(2,1)} custom-call(bf16[96,512]{1,0:T(8,128)(2,1)S(1)} %collective-permute-done.lo_ref, bf16[96,512]{1,0:T(8,128)(2,1)S(1)} %get-tuple-element.18.head_ref, bf16[2,96,512]{2,1,0:T(8,128)(2,1)S(1)} %get-tuple-element.19.mid_ref, bf16[96,512]{1,0:T(8,128)(2,1)S(1)} %get-tuple-element.17.tail_ref, ...), custom_call_target="tpu_custom_call" | custom-call | tf_op jit(solution)/shard_map/pallas_call | solution.py:30
  58.4 1.7 %shard_map.78 = bf16[64,4,512]{2,1,0:T(4,128)(2,1)} custom-call(bf16[96,512]{1,0:T(8,128)(2,1)S(1)} %collective-permute-done.lo_ref, bf16[96,512]{1,0:T(8,128)(2,1)S(1)} %get-tuple-element.18.head_ref, bf16[2,96,512]{2,1,0:T(8,128)(2,1)S(1)} %get-tuple-element.19.mid_ref, bf16[96,512]{1,0:T(8,128)(2,1)S(1)} %get-tuple-element.17.tail_ref, ...), custom_call_target="tpu_custom_call" | custom-call | tf_op jit(solution)/shard_map/pallas_call | solution.py:30
  60.1 3.0 %all-to-all-done.1 = f32[16,8,128]{2,1,0:T(8,128)S(1)} async-done(((f32[16,8,128]{2,1,0:T(8,128)}), f32[16,8,128]{2,1,0:T(8,128)S(1)}, u32[]{:S(2)}, u32[]{:S(2)}) %all-to-all-start.1) | async-done | bytes 65568 | tf_op jit(solution)/shard_map/all_to_all | solution.py:214
  63.1 0.1 fusion
  63.2 17.6 %all_to_all.16 = bf16[64,8,128]{2,1,0:T(8,128)(2,1)S(1)} all-to-all(bf16[64,8,128]{2,1,0:T(8,128)(2,1)S(1)} %broadcast_in_dim.23), channel_id=1, replica_groups=mesh['dp_0'=16,'dp_1'=8,'dp_2'=2,'gz'=4] {'dp_2','dp_1','gz'}, dimensions={0} | all-to-all | bytes 262144 | tf_op jit(solution)/shard_map/all_to_all | solution.py:214
  80.9 0.0 copy-start.1
  80.9 0.6 fusion.1
  81.4 0.1 copy-done.1
  (7 shorter events, 0.1 us)
Async XLA Ops:
  1.8 5.6 %collective-permute-start = (bf16[96,512]{1,0:T(8,128)(2,1)S(1)}, bf16[96,512]{1,0:T(8,128)(2,1)S(1)}, u32[]{:S(2)}, u32[]{:S(2)}) collective-permute-start(bf16[96,512]{1,0:T(8,128)(2,1)S(1)} %get-tuple-element.17.tail_ref), channel_id=1, source_target_pairs={{0,1},{1,2},{2,3},{4,5},{5,6},{6,7},{8,9},{9,10},{10,11},{12,13},{... | collective-permute-start | bytes 294920 | tf_op jit(solution)/shard_map/ppermute | solution.py:225
  8.0 14.9 %collective-permute-start.1 = (f32[2,16,8,128]{3,2,1,0:T(8,128)S(1)}, f32[2,16,8,128]{3,2,1,0:T(8,128)S(1)}, u32[]{:S(2)}, u32[]{:S(2)}) collective-permute-start(f32[2,16,8,128]{3,2,1,0:T(8,128)S(1)} %get-tuple-element.23), channel_id=1, source_target_pairs={{0,4},{4,0},{1,5},{5,1},{2,6},{6,2},{3,7},{7,3},{8,12},{12,8},{9,1... | collective-permute-start | bytes 393224 | tf_op jit(solution)/shard_map/ppermute | solution.py:230
  35.9 16.8 %copy-start = (bf16[27,2048]{1,0:T(8,128)(2,1)S(1)}, bf16[27,2048]{1,0:T(8,128)(2,1)}, u32[]{:S(2)}) copy-start(bf16[27,2048]{1,0:T(8,128)(2,1)} %param.5) | copy-start | bytes 331780
  36.6 26.5 %all-to-all-start.1 = ((f32[16,8,128]{2,1,0:T(8,128)}), f32[16,8,128]{2,1,0:T(8,128)S(1)}, u32[]{:S(2)}, u32[]{:S(2)}) async-start(f32[16,8,128]{2,1,0:T(8,128)} %broadcast_in_dim.19), calls=%async_computation.1 | async-start | bytes 131072 | tf_op jit(solution)/shard_map/all_to_all | solution.py:214
  51.4 5.4 %collective-permute-start.2 = (bf16[96,512]{1,0:T(8,128)(2,1)S(1)}, bf16[96,512]{1,0:T(8,128)(2,1)S(1)}, u32[]{:S(2)}, u32[]{:S(2)}) collective-permute-start(bf16[96,512]{1,0:T(8,128)(2,1)S(1)} %get-tuple-element.18.head_ref), channel_id=1, source_target_pairs={{1,0},{2,1},{3,2},{5,4},{6,5},{7,6},{9,8},{10,9},{11,10},{13,12},{... | collective-permute-start | bytes 294920 | tf_op jit(solution)/shard_map/ppermute | solution.py:226
  53.7 0.7 copy-start.2
  80.9 0.7 copy-start.1
